TPU v7x, 32 devices: a whole 2x2x4 slice. The times are simulated.
32 devices in a mesh: parts: 2 (over x), tile: 16 (over z, y, core).
Axes of the slice: x: 2, y: 2, z: 4, core: 2. Of those that a mesh axis runs over, the one named last changes fastest.
Arguments:
- src_slots: bfloat16 [32, 512, 512], P(('parts', 'tile')), parts along dimension 0, may hold values from -6 to 6
- v_tiles: bfloat16 [32, 16, 512, 256], P(('parts', 'tile')), parts along dimension 0, may hold values from -0.1875 to 0.1875
- u_tiles: bfloat16 [32, 16, 256, 512], P(('parts', 'tile')), parts along dimension 0, may hold values from -0.125 to 0.125
- ranks: int32 [2, 16, 16], P('parts'), parts along dimension 0, may hold values from 16 to 128, as said below
- col_map: int32 [2, 16], P('parts'), parts along dimension 0, may hold values from 0 to 15, each once within a row
- gate_start: int32 [32, 512], P('parts', 'tile'), parts along dimension 0, may hold values from 0 to 960
Outputs:
- image: bfloat16 [32, 512, 64, 256], P('parts', 'tile'), parts along dimension 0
There are 2 independent parts, one for each index of `parts`. A program takes and returns all parts, laid end to end along the dimension named above; each array names one. Nothing has to cross between parts.
Inputs may be any that keep to these rules, and one draw needn't show every extreme that they name: `ranks`: each rank is a multiple of 16; the columns of V and U from a tile's rank on are not part of the tile. `col_map`: each row f is a permutation of the tile columns.
All inputs are finite; a program needn't handle non-finite values.
Results may differ from a plain program's by a relative error of at most 0.008.
Values may be sent and summed in bfloat16 or wider, within the bound.
No kernel may reach another device: no remote copies, remote signals or barrier semaphores. Data moves between devices by JAX's collectives and lax.ppermute only.
A program may use at most 192 MiB of HBM per device.

v0:
```python
import math

import jax
import jax.numpy as jnp
from jax import lax
from jax.sharding import PartitionSpec as P

TC = 16
TR = 16
RMAX = 128
SIDE = 16
NT = 1024
GT = 64


edge_weight = 0.15
centre_weight = 0.7


def gated_trace(real_part, imag_part, gate_start, freq_count, samples, gate_len):
    sample_times = gate_start[:, :, None] + jnp.arange(gate_len, dtype=jnp.int32)[None, None, :]
    bin_index = 4 + jnp.arange(freq_count, dtype=jnp.int32) * (samples // (2 * freq_count))
    phases = bin_index[:, None, None, None] * sample_times[None] % samples
    angles = phases.astype(jnp.float32) * (2.0 * math.pi / samples)
    summed = jnp.einsum(
        "firs,firt->irts", real_part, jnp.cos(angles), precision=lax.Precision.HIGHEST
    )
    summed = summed - jnp.einsum(
        "firs,firt->irts", imag_part, jnp.sin(angles), precision=lax.Precision.HIGHEST
    )
    return summed * (2.0 / math.sqrt(freq_count))


def smooth_grid(signal, grid_side):
    grid_width = signal.shape[-1]
    column = jnp.arange(grid_width) % grid_side
    zeros_one = jnp.zeros(signal.shape[:-1] + (1,), signal.dtype)
    before = jnp.concatenate([zeros_one, signal[..., :-1]], axis=-1)
    before = jnp.where(column == 0, 0.0, before)
    after = jnp.concatenate([signal[..., 1:], zeros_one], axis=-1)
    after = jnp.where(column == grid_side - 1, 0.0, after)
    across = centre_weight * signal + edge_weight * (before + after)
    zeros_row = jnp.zeros(signal.shape[:-1] + (grid_side,), signal.dtype)
    above = jnp.concatenate([zeros_row, across[..., :-grid_side]], axis=-1)
    below = jnp.concatenate([across[..., grid_side:], zeros_row], axis=-1)
    return centre_weight * across + edge_weight * (above + below)


def on_device(src_slots, v_tiles, u_tiles, ranks, col_map, gate_start):
    devices = lax.axis_size("tile")
    device = lax.axis_index("tile")
    freq_count = devices // TC
    blocks_per = devices // TR
    rank_block = RMAX // blocks_per
    sources = src_slots.shape[-1] // 2
    tile_len = v_tiles.shape[2]
    receivers = tile_len // devices
    frequency = device // TC
    slot_here = device % TC
    column_ids = jnp.arange(TC, dtype=jnp.int32)
    freq_ids = jnp.arange(freq_count, dtype=jnp.int32)
    slot_rows = (freq_ids[:, None] == frequency) & (column_ids[None, :] == slot_here)
    column = jnp.sum(jnp.where(slot_rows, col_map, 0))
    picker = (freq_ids[:, None, None] == frequency) & (column_ids[None, None, :] == column)
    rank_rows = jnp.sum(jnp.where(picker, ranks, 0), axis=(0, 2))
    product = jnp.einsum(
        "ibr,bs->irs", v_tiles[0], src_slots[0], preferred_element_type=jnp.float32
    )
    real_z = product[:, :RMAX, :sources] - product[:, RMAX:, sources:]
    imag_z = product[:, :RMAX, sources:] + product[:, RMAX:, :sources]
    live_rows = jnp.arange(RMAX, dtype=jnp.int32)[None, :, None] < rank_rows[:, None, None]
    reduced = jnp.where(live_rows, jnp.concatenate([real_z, imag_z], axis=-1), 0.0).astype(
        jnp.bfloat16
    )
    outgoing = reduced.reshape(devices, rank_block, 2 * sources)
    incoming = lax.all_to_all(outgoing, "tile", split_axis=0, concat_axis=0, tiled=True)
    incoming = incoming.reshape(freq_count, TC, rank_block, 2 * sources)
    mapping = (col_map[:, :, None] == column_ids[None, None, :]).astype(jnp.bfloat16)
    by_column = jnp.einsum(
        "fxj,fxqs->fjqs", mapping, incoming, preferred_element_type=jnp.float32
    ).astype(jnp.bfloat16)
    swapped = jnp.concatenate([-by_column[..., sources:], by_column[..., :sources]], axis=-1)
    stacked = jnp.concatenate([by_column, swapped], axis=2)
    weights = u_tiles[0].reshape(freq_count, TC, 2 * rank_block, tile_len)
    partial_value = jnp.einsum(
        "fjcb,fjcs->fbs", weights, stacked, preferred_element_type=jnp.float32
    ).astype(jnp.bfloat16)
    spread = partial_value.reshape(freq_count, devices, receivers, 2, sources)
    arrived = lax.all_to_all(spread, "tile", split_axis=1, concat_axis=1, tiled=True)
    summed = (
        arrived.reshape(freq_count, TR, blocks_per, arrived.shape[2], 2, arrived.shape[4])
        .astype(jnp.float32)
        .sum(axis=2)
    )
    traces = gated_trace(
        summed[:, :, :, 0, :], summed[:, :, :, 1, :], gate_start, freq_count, NT, GT
    )
    return smooth_grid(traces, SIDE).astype(jnp.bfloat16)


def solution(mesh):
    placed = (
        P(("parts", "tile"), None, None),
        P(("parts", "tile"), None, None, None),
        P(("parts", "tile"), None, None, None),
        P("parts", None, None),
        P("parts", None),
        P("parts", "tile"),
    )
    return jax.shard_map(
        on_device,
        mesh=mesh,
        in_specs=placed,
        out_specs=P("parts", "tile", None, None),
        check_vma=False,
    )
```

profile of v0, /device:TPU:0, one launch (start us, length us, event | category | flops | bytes accessed | tf_op | source)
XLA Modules:
  0.0 265.1 jit_solution(12622137564884940920)
XLA Ops:
  0.0 1.4 fusion.32
  1.5 0.7 compare_and_fusion
  2.1 0.8 select_reduce_fusion
  2.9 0.1 iota_compare_fusion
  3.0 4.6 %fusion.7 = f32[16,256,512]{2,1,0:T(8,128)S(1)} fusion(bf16[1,16,512,256]{3,2,1,0:T(8,128)(2,1)} %param.7, bf16[1,512,512]{2,1,0:T(8,128)(2,1)S(1)} %copy-done), kind=kOutput, calls=%fused_computation.12 | convolution fusion | flops 2147483648 | bytes 13107200 | tf_op jit(solution)/shard_map/ibr,bs->irs/dot_general | solution.py:66
  7.6 0.7 slice_subtract_fusion
  8.2 0.7 fusion.1
  9.0 54.4 %all_to_all.10 = bf16[16,128,512]{2,1,0:T(8,128)(2,1)S(1)} all-to-all(bf16[16,128,512]{2,1,0:T(8,128)(2,1)S(1)} %fusion.1), channel_id=1, replica_groups=mesh['parts'=2,'tile'=16] {'tile'}, dimensions={0} | all-to-all | bytes 4194304 | tf_op jit(solution)/shard_map/all_to_all | solution.py:76
  63.4 1.3 convert_bitcast_fusion
  64.7 0.1 slice_negate_fusion
  64.9 0.0 copy-start.2
  64.9 3.1 %fusion.20 = bf16[512,512]{0,1:T(8,128)(2,1)S(1)} fusion(bf16[16,256,512]{2,1,0:T(8,128)(2,1)S(1)} %bitcast.37, bf16[1,16,128,256]{3,1,2,0:T(8,128)(2,1)S(1)} %get-tuple-element.12, bf16[1,16,128,256]{3,1,2,0:T(8,128)(2,1)S(1)} %get-tuple-element.11, bf16[1,16,128,512]{3,1,2,0:T(8,128)(2,1)S(1)} %convert_bitcast_fusion), kind=kOutput, calls=%fused_computation.22 | convolution fusion | flops 2160328704 | bytes 8912896 | tf_op jit(solution)/shard_map/fjcb,fjcs->fbs/dot_general | solution.py:85
  67.9 0.2 copy.19
  68.2 0.9 reshape.137
  69.1 5.2 %all-to-all-start.1 = ((bf16[1,16,32,2,256]{4,3,2,0,1:T(2,128)(2,1)}), bf16[1,16,32,2,256]{4,3,2,0,1:T(2,128)(2,1)S(1)}, u32[]{:S(2)}, u32[]{:S(2)}) async-start(bf16[1,16,32,2,256]{4,3,2,0,1:T(2,128)(2,1)} %bitcast.10), calls=%async_computation.1 | async-start | bytes 1048576 | tf_op jit(solution)/shard_map/all_to_all | solution.py:89
  74.3 1.1 fusion.28
  75.4 13.1 %all-to-all-done.1 = bf16[1,16,32,2,256]{4,3,2,0,1:T(2,128)(2,1)S(1)} async-done(((bf16[1,16,32,2,256]{4,3,2,0,1:T(2,128)(2,1)}), bf16[1,16,32,2,256]{4,3,2,0,1:T(2,128)(2,1)S(1)}, u32[]{:S(2)}, u32[]{:S(2)}) %all-to-all-start.1) | async-done | bytes 524320 | tf_op jit(solution)/shard_map/all_to_all | solution.py:89
  88.5 1.1 slice_convert_fusion.1
  89.6 0.1 copy_bitcast_fusion
  89.7 11.7 %fusion = f32[16,32,64,256]{3,2,1,0:T(8,128)} fusion(f32[16,32,256]{2,1,0:T(8,128)S(1)} %get-tuple-element.17, f32[16,32,64]{2,1,0:T(8,128)S(1)} %get-tuple-element.16, f32[16,32,256]{2,1,0:T(8,128)S(1)} %get-tuple-element.18, f32[16,32,64]{2,1,0:T(8,128)S(1)} %get-tuple-element.15), kind=kLoop, calls=%fused_computation.3 | loop fusion | flops 33554432 | bytes 34865152 | tf_op jit(solution)/shard_map/mul | solution.py:31
  101.4 45.9 %fusion.35 = (f32[16,32,64,255]{3,2,1,0:T(8,128)}, f32[16,32,64,255]{3,2,1,0:T(8,128)}) fusion(f32[16,32,64,256]{3,2,1,0:T(8,128)} %fusion), kind=kLoop, calls=%fused_computation.50 | loop fusion | bytes 133693440 | tf_op jit(solution)/shard_map/slice | solution.py:38
  147.3 33.8 %multiply_add_fusion = f32[16,32,64,256]{3,2,1,0:T(8,128)} fusion(f32[16,32,64,255]{3,2,1,0:T(8,128)} %get-tuple-element.8, f32[16,32,64,255]{3,2,1,0:T(8,128)} %get-tuple-element.7, f32[16,32,256]{2,1,0:T(8,128)S(1)} %get-tuple-element.17, f32[16,32,64]{2,1,0:T(8,128)S(1)} %get-tuple-element.16, f32[16,32,256]{2,1,0:T(8,128)S(1)} %get-tuple-element.18, ...), kind=kLoop, calls=%fused_computation.1 | loop fusion | flops 75497472 | bytes 101712384 | tf_op jit(solution)/shard_map/add | solution.py:42
  181.1 45.9 %fusion.34 = (f32[16,32,64,240]{3,2,1,0:T(8,128)}, f32[16,32,64,240]{3,2,1,0:T(8,128)}) fusion(f32[16,32,64,256]{3,2,1,0:T(8,128)} %multiply_add_fusion), kind=kLoop, calls=%fused_computation.49 | loop fusion | bytes 125829120 | tf_op jit(solution)/shard_map/slice | solution.py:44
  227.0 38.1 %add_convert_fusion = bf16[16,32,64,256]{3,2,1,0:T(8,128)(2,1)} fusion(f32[16,32,64,240]{3,2,1,0:T(8,128)} %get-tuple-element.6, f32[16,32,64,240]{3,2,1,0:T(8,128)} %get-tuple-element.5, f32[16,32,64,256]{3,2,1,0:T(8,128)} %multiply_add_fusion), kind=kLoop, calls=%fused_computation | loop fusion | flops 41943040 | bytes 113246208 | tf_op jit(solution)/shard_map/convert_element_type | solution.py:98
  (10 shorter events, 0.0 us)
Async XLA Ops:
  0.0 3.0 %copy-start = (bf16[1,512,512]{2,1,0:T(8,128)(2,1)S(1)}, bf16[1,512,512]{2,1,0:T(8,128)(2,1)}, u32[]{:S(2)}) copy-start(bf16[1,512,512]{2,1,0:T(8,128)(2,1)} %param.6) | copy-start | bytes 1572868
  0.0 63.4 %copy-start.3 = (s32[1,16]{1,0:T(1,128)S(1)}, s32[1,16]{1,0:T(1,128)}, u32[]{:S(2)}) copy-start(s32[1,16]{1,0:T(1,128)} %param.10) | copy-start | bytes 196
  0.0 64.9 %copy-start.4 = (bf16[1,16,256,512]{3,2,1,0:T(8,128)(2,1)S(1)}, bf16[1,16,256,512]{3,2,1,0:T(8,128)(2,1)}, u32[]{:S(2)}) copy-start(bf16[1,16,256,512]{3,2,1,0:T(8,128)(2,1)} %param.8) | copy-start | bytes 12582916
  64.9 9.4 %copy-start.2 = (s32[16,32]{1,0:T(8,128)S(1)}, s32[16,32]{1,0:T(8,128)}, u32[]{:S(2)}) copy-start(s32[16,32]{1,0:T(8,128)} %param.11) | copy-start | bytes 6148
  69.1 19.4 %all-to-all-start.1 = ((bf16[1,16,32,2,256]{4,3,2,0,1:T(2,128)(2,1)}), bf16[1,16,32,2,256]{4,3,2,0,1:T(2,128)(2,1)S(1)}, u32[]{:S(2)}, u32[]{:S(2)}) async-start(bf16[1,16,32,2,256]{4,3,2,0,1:T(2,128)(2,1)} %bitcast.10), calls=%async_computation.1 | async-start | bytes 1048576 | tf_op jit(solution)/shard_map/all_to_all | solution.py:89
  227.0 38.1 %copy-start.1 = (bf16[1,512,512]{2,1,0:T(8,128)(2,1)S(1)}, bf16[1,512,512]{2,1,0:T(8,128)(2,1)}, u32[]{:S(2)}) copy-start(bf16[1,512,512]{2,1,0:T(8,128)(2,1)} %param.6) | copy-start | bytes 1572868
where the time goes:
time: 265 us
  local copies, waits for them, and re-layouts  93 us (35%)
  other arithmetic  90.3 us (34%)
  blocking collectives  54.4 us (21%)
  waiting for transfers between devices  13.1 us (5%)
  matrix products  8.97 us (3%)
  starting transfers between devices  5.15 us (2%)
    all_to_all x1, blocking collectives, on_device(): lax.all_to_all(outgoing, 'tile', split_axis=0, concat_axis=0, tiled=True)  54.4 us
    slice x1, local copies, waits for them, and re-layouts, smooth_grid(): before = jnp.concatenate([zeros_one, signal[..., :-1]], axis=-1)  45.9 us
    slice x1, local copies, waits for them, and re-layouts, smooth_grid(): above = jnp.concatenate([zeros_row, across[..., :-grid_side]], axis=-1)  45.9 us
    convert_element_type x1, other arithmetic, on_device(): return smooth_grid(traces, SIDE).astype(jnp.bfloat16)  38.1 us
    add x1, other arithmetic, smooth_grid(): across = centre_weight * signal + edge_weight * (before + after)  33.8 us
    all_to_all x1, waiting for transfers between devices, on_device(): lax.all_to_all(spread, 'tile', split_axis=1, concat_axis=1, tiled=True)  13.1 us
    mul x1, other arithmetic, gated_trace(): return summed * (2.0 / math.sqrt(freq_count))  11.7 us
  transfers between devices with their start and end apart: 1, of which 1 were waited for; matrix products, arithmetic and copies ran while one was open for 0% of the time, Pallas kernels for 0%

commit v1 on v0

v1 whole, which is shorter than its diff:
```python
import functools
import math

import jax
import jax.numpy as jnp
from jax import lax
from jax.experimental import pallas as pl
from jax.experimental.pallas import tpu as pltpu
from jax.sharding import PartitionSpec as P

TC = 16
TR = 16
RMAX = 128
SIDE = 16
NT = 1024
GT = 64

edge_weight = 0.15
centre_weight = 0.7


def over_rows(left, right):
    return lax.dot_general(
        left, right, (((0,), (0,)), ((), ())), preferred_element_type=jnp.float32
    )


def project_kernel(rank_ref, v_ref, x_ref, z_ref):
    tiles = v_ref.shape[0]
    sources = x_ref.shape[-1] // 2
    first = pl.program_id(0) * tiles
    row = lax.broadcasted_iota(jnp.int32, (RMAX, 2 * sources), 0)
    for t in range(tiles):
        product = over_rows(v_ref[t], x_ref[0])
        real_z = product[:RMAX, :sources] - product[RMAX:, sources:]
        imag_z = product[:RMAX, sources:] + product[RMAX:, :sources]
        both = jnp.concatenate([real_z, imag_z], axis=-1)
        z_ref[t] = jnp.where(row < rank_ref[first + t], both, 0.0).astype(jnp.bfloat16)


def project(rank_rows, v_tiles, src_slots, tiles):
    _, rows, tile_len, wide = v_tiles.shape
    cols = src_slots.shape[-1]
    return pl.pallas_call(
        project_kernel,
        out_shape=jax.ShapeDtypeStruct((rows, RMAX, cols), jnp.bfloat16),
        grid_spec=pltpu.PrefetchScalarGridSpec(
            num_scalar_prefetch=1,
            grid=(rows // tiles,),
            in_specs=[
                pl.BlockSpec((None, tiles, tile_len, wide), lambda i, r: (0, i, 0, 0)),
                pl.BlockSpec((1, tile_len, cols), lambda i, r: (0, 0, 0)),
            ],
            out_specs=pl.BlockSpec((tiles, RMAX, cols), lambda i, r: (i, 0, 0)),
        ),
        name="project",
    )(rank_rows, v_tiles, src_slots)


def expand_kernel(col_ref, z_ref, u_ref, y_ref, acc_ref):
    f = pl.program_id(0)
    sources = z_ref.shape[-1] // 2
    for x in range(TC):
        z = z_ref[x]
        swapped = jnp.concatenate([-z[:, sources:], z[:, :sources]], axis=-1)
        stacked = jnp.concatenate([z, swapped], axis=0)
        term = over_rows(u_ref[col_ref[f, x]], stacked)
        if x == 0:
            acc_ref[...] = term
        else:
            acc_ref[...] += term
    y_ref[...] = acc_ref[...].astype(jnp.bfloat16)


def expand(col_map, incoming, u_tiles):
    freq_count = col_map.shape[0]
    _, rank_block, cols = incoming.shape
    tile_len = u_tiles.shape[-1]
    incoming = incoming.reshape(freq_count, TC, rank_block, cols)
    weights = u_tiles.reshape(freq_count, TC, 2 * rank_block, tile_len)
    return pl.pallas_call(
        expand_kernel,
        out_shape=jax.ShapeDtypeStruct((freq_count, tile_len, cols), jnp.bfloat16),
        grid_spec=pltpu.PrefetchScalarGridSpec(
            num_scalar_prefetch=1,
            grid=(freq_count,),
            in_specs=[
                pl.BlockSpec((None, TC, rank_block, cols), lambda f, c: (f, 0, 0, 0)),
                pl.BlockSpec((None, TC, 2 * rank_block, tile_len), lambda f, c: (f, 0, 0, 0)),
            ],
            out_specs=pl.BlockSpec((None, tile_len, cols), lambda f, c: (f, 0, 0)),
            scratch_shapes=[pltpu.VMEM((tile_len, cols), jnp.float32)],
        ),
        name="expand",
    )(col_map, incoming, weights)


def smooth(signal):
    width = signal.shape[-1]
    place = lax.broadcasted_iota(jnp.int32, signal.shape, 1)
    column = place % SIDE
    before = jnp.where(column == 0, 0.0, pltpu.roll(signal, 1, axis=1))
    after = jnp.where(column == SIDE - 1, 0.0, pltpu.roll(signal, width - 1, axis=1))
    across = centre_weight * signal + edge_weight * (before + after)
    above = jnp.where(place < SIDE, 0.0, pltpu.roll(across, SIDE, axis=1))
    below = jnp.where(place >= width - SIDE, 0.0, pltpu.roll(across, width - SIDE, axis=1))
    return centre_weight * across + edge_weight * (above + below)


def gate_kernel(y_ref, cos_g_ref, sin_g_ref, cos_t_ref, sin_t_ref, out_ref, a_ref, b_ref):
    freq_count, blocks, receivers, cols = y_ref.shape
    sources = cols // 2
    lanes = cos_t_ref.shape[-1]
    for f in range(freq_count):
        summed = y_ref[f, 0].astype(jnp.float32)
        for k in range(1, blocks):
            summed = summed + y_ref[f, k].astype(jnp.float32)
        real_y = smooth(summed[:, :sources])
        imag_y = smooth(summed[:, sources:])
        cos_g = cos_g_ref[f]
        sin_g = sin_g_ref[f]
        a_ref[f] = cos_g * real_y - sin_g * imag_y
        b_ref[f] = sin_g * real_y + cos_g * imag_y

    for r in range(receivers):
        for start in range(0, sources, lanes):
            total = None
            for f in range(freq_count):
                a = a_ref[f, r:r + 1, start:start + lanes]
                b = b_ref[f, r:r + 1, start:start + lanes]
                term = cos_t_ref[f] * a - sin_t_ref[f] * b
                total = term if total is None else total + term
            out_ref[r, :, start:start + lanes] = total.astype(out_ref.dtype)


def gate(arrived, cos_g, sin_g, cos_t, sin_t):
    freq_count, rows, blocks, receivers, cols = arrived.shape
    sources = cols // 2
    gate_len, lanes = cos_t.shape[1:]
    whole = lambda i: (0, 0, 0)
    return pl.pallas_call(
        gate_kernel,
        out_shape=jax.ShapeDtypeStruct((rows, receivers, gate_len, sources), jnp.bfloat16),
        grid=(rows,),
        in_specs=[
            pl.BlockSpec((freq_count, None, blocks, receivers, cols), lambda i: (0, i, 0, 0, 0)),
            pl.BlockSpec((freq_count, None, receivers, 1), lambda i: (0, i, 0, 0)),
            pl.BlockSpec((freq_count, None, receivers, 1), lambda i: (0, i, 0, 0)),
            pl.BlockSpec((freq_count, gate_len, lanes), whole),
            pl.BlockSpec((freq_count, gate_len, lanes), whole),
        ],
        out_specs=pl.BlockSpec((None, receivers, gate_len, sources), lambda i: (i, 0, 0, 0)),
        scratch_shapes=[pltpu.VMEM((freq_count, receivers, sources), jnp.float32)] * 2,
        name="gate",
    )(arrived, cos_g, sin_g, cos_t, sin_t)


def waves(times, bins):
    phases = bins.reshape((-1,) + (1,) * times.ndim) * times[None] % NT
    angles = phases.astype(jnp.float32) * (2.0 * math.pi / NT)
    return jnp.cos(angles), jnp.sin(angles)


def on_device(src_slots, v_tiles, u_tiles, ranks, col_map, gate_start):
    devices = lax.axis_size("tile")
    device = lax.axis_index("tile")
    freq_count = devices // TC
    blocks_per = devices // TR
    rank_block = RMAX // blocks_per
    cols = src_slots.shape[-1]
    tile_len = v_tiles.shape[2]
    receivers = tile_len // devices
    column_ids = jnp.arange(TC, dtype=jnp.int32)
    freq_ids = jnp.arange(freq_count, dtype=jnp.int32)
    slot_rows = (freq_ids[:, None] == device // TC) & (column_ids[None, :] == device % TC)
    mine = jnp.sum(
        jnp.where(slot_rows[:, :, None] & (col_map[:, :, None] == column_ids), 1, 0), axis=1
    )
    rank_rows = jnp.sum(ranks * mine[:, None, :], axis=(0, 2))

    reduced = project(rank_rows, v_tiles, src_slots, 2)
    outgoing = reduced.reshape(devices, rank_block, cols)
    incoming = lax.all_to_all(outgoing, "tile", split_axis=0, concat_axis=0, tiled=True)
    partial_value = expand(col_map, incoming, u_tiles)
    spread = partial_value.reshape(freq_count, devices, receivers, cols)
    arrived = lax.all_to_all(spread, "tile", split_axis=1, concat_axis=1, tiled=True)
    arrived = arrived.reshape(freq_count, TR, blocks_per, receivers, cols)

    bins = 4 + freq_ids * (NT // (2 * freq_count))
    scale = 2.0 / math.sqrt(freq_count)
    cos_g, sin_g = waves(gate_start, bins)
    cos_t, sin_t = waves(jnp.arange(GT, dtype=jnp.int32), bins)
    lanes = min(128, cols // 2)
    cos_t, sin_t = (
        jnp.broadcast_to(wave[:, :, None], wave.shape + (lanes,)) for wave in (cos_t, sin_t)
    )
    return gate(arrived, scale * cos_g[..., None], scale * sin_g[..., None], cos_t, sin_t)


def solution(mesh):
    placed = (
        P(("parts", "tile"), None, None),
        P(("parts", "tile"), None, None, None),
        P(("parts", "tile"), None, None, None),
        P("parts", None, None),
        P("parts", None),
        P("parts", "tile"),
    )
    return jax.shard_map(
        on_device,
        mesh=mesh,
        in_specs=placed,
        out_specs=P("parts", "tile", None, None),
        check_vma=False,
    )
```

time: 265 us -> 109 us (0.41)
  local copies, waits for them, and re-layouts: 93 us -> 3.22 us
  other arithmetic: 90.3 us -> 2.31 us
  Pallas kernels: 0 us -> 29.4 us
  matrix products: 8.97 us -> 0 us
    slice x2 -> x0, local copies, waits for them, and re-layouts: 91.8 us -> none  [the longest x1 45.9 us: smooth_grid(): before = jnp.concatenate([zeros_one, signal[..., :-1]], axis=-1)]
    convert_element_type x2 -> x0, other arithmetic: 38.8 us -> none  [the longest x1 38.1 us: on_device(): return smooth_grid(traces, SIDE).astype(jnp.bfloat16)]
    add x1 -> x0, other arithmetic: 33.8 us -> none  [smooth_grid(): across = centre_weight * signal + edge_weight * (before + after)]
    pallas_call x0 -> x3, Pallas kernels: none -> 29.4 us  [the longest x1 13.9 us: gate(): pl.pallas_call(gate_kernel, out_shape=jax.ShapeDtypeStruct((rows, receive...]
    mul x1, other arithmetic: 11.7 us -> 0.06 us  [on_device(): scale * sin_g[..., None]]
    dot_general x3 -> x0, matrix products: 8.97 us -> none  [the longest x1 4.58 us: on_device(): jnp.einsum('ibr,bs->irs', v_tiles[0], src_slots[0], preferred_element_typ...]
  transfers between devices with their start and end apart: 1 -> 1, of which waited for: 1 -> 1; matrix products, arithmetic and copies ran while one was open for 0% -> 2% of each run, Pallas kernels for 0% -> 0%
where the time goes in v1:
time: 109 us; the launch traced here: 107 us
  blocking collectives  54.7 us (50%)
  Pallas kernels  29.4 us (27%)
  waiting for transfers between devices  12.3 us (11%)
  starting transfers between devices  5.14 us (5%)
  local copies, waits for them, and re-layouts  3.22 us (3%)
  other arithmetic  2.31 us (2%)
    all_to_all x1, blocking collectives, on_device(): lax.all_to_all(outgoing, 'tile', split_axis=0, concat_axis=0, tiled=True)  54.7 us
    pallas_call x1, Pallas kernels, gate(): pl.pallas_call(gate_kernel, out_shape=jax.ShapeDtypeStruct((rows, receive...  13.9 us
    all_to_all x1, waiting for transfers between devices, on_device(): lax.all_to_all(spread, 'tile', split_axis=1, concat_axis=1, tiled=True)  12.3 us
    pallas_call x1, Pallas kernels, project(): pl.pallas_call(project_kernel, out_shape=jax.ShapeDtypeStruct((rows, RMAX...  8.68 us
    pallas_call x1, Pallas kernels, expand(): pl.pallas_call(expand_kernel, out_shape=jax.ShapeDtypeStruct((freq_count,...  6.77 us
    all_to_all x1, starting transfers between devices, on_device(): lax.all_to_all(spread, 'tile', split_axis=1, concat_axis=1, tiled=True)  5.14 us
  transfers between devices with their start and end apart: 1, of which 1 were waited for; matrix products, arithmetic and copies ran while one was open for 2% of the time, Pallas kernels for 0%

profile of v1, /device:TPU:0, one launch (start us, length us, event | category | flops | bytes accessed | tf_op | source)
XLA Modules:
  0.0 107.1 jit_solution(5759019495453741871)
XLA Ops:
  0.0 0.7 select_reduce_fusion
  0.8 1.4 %multiply_reduce_fusion.rank_ref = s32[16]{0:T(128)} fusion(s32[1,16,16]{2,1,0:T(8,128)} %param.9, s32[16]{0:T(128)S(1)} %select_reduce_fusion), kind=kLoop, calls=%fused_computation.8 | loop fusion | flops 496 | bytes 1152 | tf_op jit(solution)/shard_map/reduce_sum | solution.py:179
  2.2 8.7 %project.1 = bf16[16,128,512]{2,1,0:T(8,128)(2,1)} custom-call(s32[16]{0:T(128)} %multiply_reduce_fusion.rank_ref, bf16[1,16,512,256]{3,2,1,0:T(8,128)(2,1)} %v_ref.1, bf16[1,512,512]{2,1,0:T(8,128)(2,1)} %x_ref.1), custom_call_target="tpu_custom_call" | custom-call | tf_op jit(solution)/shard_map/project/pallas_call | solution.py:44
  10.8 54.7 %all_to_all.10 = bf16[16,128,512]{2,1,0:T(8,128)(2,1)} all-to-all(bf16[16,128,512]{2,1,0:T(8,128)(2,1)} %project.1), channel_id=1, replica_groups=mesh['parts'=2,'tile'=16] {'tile'}, dimensions={0} | all-to-all | bytes 4194304 | tf_op jit(solution)/shard_map/all_to_all | solution.py:183
  65.5 0.0 copy-start.1
  65.5 6.8 %expand.1 = bf16[1,512,512]{2,1,0:T(8,128)(2,1)} custom-call(s32[1,16]{1,0:T(1,128)} %col_ref.1, bf16[1,16,128,512]{3,2,1,0:T(8,128)(2,1)} %bitcast.10, bf16[1,16,256,512]{3,2,1,0:T(8,128)(2,1)} %u_ref.1), custom_call_target="tpu_custom_call" | custom-call | tf_op jit(solution)/shard_map/expand/pallas_call | solution.py:81
  72.3 5.1 %all-to-all-start.1 = ((bf16[1,16,32,512]{3,2,0,1:T(8,128)(2,1)}), bf16[1,16,32,512]{3,2,0,1:T(8,128)(2,1)S(1)}, u32[]{:S(2)}, u32[]{:S(2)}) async-start(bf16[1,16,32,512]{3,2,0,1:T(8,128)(2,1)} %bitcast.12), calls=%async_computation.1 | async-start | bytes 1048576 | tf_op jit(solution)/shard_map/all_to_all | solution.py:186
  77.4 0.0 copy-done.1
  77.4 0.1 multiply_bitcast_fusion
  77.5 0.9 copy.16.sin_g_ref
  78.4 0.9 copy.15.cos_g_ref
  79.3 0.1 fusion.8
  79.3 0.1 fusion.7
  79.4 12.3 %all-to-all-done.1 = bf16[1,16,32,512]{3,2,0,1:T(8,128)(2,1)S(1)} async-done(((bf16[1,16,32,512]{3,2,0,1:T(8,128)(2,1)}), bf16[1,16,32,512]{3,2,0,1:T(8,128)(2,1)S(1)}, u32[]{:S(2)}, u32[]{:S(2)}) %all-to-all-start.1) | async-done | bytes 524320 | tf_op jit(solution)/shard_map/all_to_all | solution.py:186
  91.7 0.0 copy-start
  91.7 0.8 broadcast_in_dim.15.sin_t_ref
  92.5 0.7 broadcast_in_dim.14.cos_t_ref
  93.1 0.0 copy-done
  93.2 13.9 %gate.1 = bf16[16,32,64,256]{3,2,1,0:T(8,128)(2,1)} custom-call(bf16[1,16,1,32,512]{4,3,2,1,0:T(8,128)(2,1)} %bitcast.11, f32[1,16,32,1]{3,2,1,0:T(8,128)} %copy.15.cos_g_ref, f32[1,16,32,1]{3,2,1,0:T(8,128)} %copy.16.sin_g_ref, f32[1,64,128]{2,1,0:T(8,128)} %broadcast_in_dim.14.cos_t_ref, f32[1,64,128]{2,1,0:T(8,128)} %broadcast_in_dim.15.sin_t_ref), custom_call_target="tpu_custom_call" | custom-call | tf_op jit(solution)/shard_map/gate/pallas_call | solution.py:141
  (1 shorter events, 0.0 us)
Async XLA Ops:
  65.5 11.9 %copy-start.1 = (s32[16,32]{1,0:T(8,128)S(1)}, s32[16,32]{1,0:T(8,128)}, u32[]{:S(2)}) copy-start(s32[16,32]{1,0:T(8,128)} %param.11) | copy-start | bytes 6148
  72.3 19.4 %all-to-all-start.1 = ((bf16[1,16,32,512]{3,2,0,1:T(8,128)(2,1)}), bf16[1,16,32,512]{3,2,0,1:T(8,128)(2,1)S(1)}, u32[]{:S(2)}, u32[]{:S(2)}) async-start(bf16[1,16,32,512]{3,2,0,1:T(8,128)(2,1)} %bitcast.12), calls=%async_computation.1 | async-start | bytes 1048576 | tf_op jit(solution)/shard_map/all_to_all | solution.py:186
  91.7 1.4 %copy-start = (bf16[1,16,32,512]{3,2,0,1:T(8,128)(2,1)}, bf16[1,16,32,512]{3,2,0,1:T(8,128)(2,1)S(1)}, u32[]{:S(2)}) copy-start(bf16[1,16,32,512]{3,2,0,1:T(8,128)(2,1)S(1)} %all-to-all-done.1) | copy-start | bytes 1572868

commit v2 on v0

v2 whole, which is shorter than its diff:
```python
import math

import jax
import jax.numpy as jnp
from jax import lax
from jax.experimental import pallas as pl
from jax.experimental.pallas import tpu as pltpu
from jax.sharding import PartitionSpec as P

TC = 16
TR = 16
RMAX = 128
SIDE = 16
NT = 1024
GT = 64

edge_weight = 0.15
centre_weight = 0.7


def matmul(left, right, left_dim=1):
    return lax.dot_general(
        left, right, (((left_dim,), (0,)), ((), ())), preferred_element_type=jnp.float32
    )


def project_kernel(turned, rank_ref, col_ref, v_ref, x_ref, z_ref, left_ref):
    tiles, tile_len, _ = v_ref.shape
    sources = x_ref.shape[-1] // 2
    device = lax.axis_index("tile")
    freq, slot = device // TC, device % TC
    column = col_ref[freq, slot]

    @pl.when(pl.program_id(0) == 0)
    def _():
        real_x = x_ref[0, :, :sources].T
        imag_x = x_ref[0, :, sources:].T
        left_ref[:sources, :tile_len] = real_x
        left_ref[:sources, tile_len:] = -imag_x
        left_ref[sources:, :tile_len] = imag_x
        left_ref[sources:, tile_len:] = real_x

    first = pl.program_id(0) * tiles
    lane = lax.broadcasted_iota(jnp.int32, (1, 2 * RMAX), 1)
    for t in range(0, tiles, 2):
        one, two = v_ref[t], v_ref[t + 1]
        real_v = jnp.concatenate([one[:, :RMAX], two[:, :RMAX]], axis=1)
        imag_v = jnp.concatenate([one[:, RMAX:], two[:, RMAX:]], axis=1)
        both = matmul(left_ref[...], jnp.concatenate([real_v, imag_v], axis=0))
        rank_one = rank_ref[freq, first + t, column]
        rank_two = rank_ref[freq, first + t + 1, column] + RMAX
        live = (lane < rank_one) | ((lane >= RMAX) & (lane < rank_two))
        both = jnp.where(live, both, 0.0).astype(jnp.bfloat16)
        for side in range(2):
            z = both[:, side * RMAX:(side + 1) * RMAX]
            z_ref[t + side] = z if turned else z.T


def project(ranks, col_map, v_tiles, src_slots, tiles, turned):
    _, rows, tile_len, wide = v_tiles.shape
    cols = src_slots.shape[-1]
    shape = (cols, RMAX) if turned else (RMAX, cols)
    return pl.pallas_call(
        lambda *refs: project_kernel(turned, *refs),
        out_shape=jax.ShapeDtypeStruct((rows,) + shape, jnp.bfloat16),
        grid=(rows // tiles,),
        in_specs=[
            pl.BlockSpec(memory_space=pltpu.SMEM),
            pl.BlockSpec(memory_space=pltpu.SMEM),
            pl.BlockSpec((None, tiles, tile_len, wide), lambda i: (0, i, 0, 0)),
            pl.BlockSpec((1, tile_len, cols), lambda i: (0, 0, 0)),
        ],
        out_specs=pl.BlockSpec((tiles,) + shape, lambda i: (i, 0, 0)),
        scratch_shapes=[pltpu.VMEM((cols, 2 * tile_len), jnp.bfloat16)],
        name="project",
    )(ranks, col_map, v_tiles, src_slots)


def expand_kernel(turned, col_ref, z_ref, u_ref, y_ref, acc_ref):
    freq_count = u_ref.shape[0]
    sources = y_ref.shape[-1] // 2
    for f in range(freq_count):
        for x in range(TC):
            z = z_ref[f, x]
            if turned:
                real_z, imag_z = z[:sources], z[sources:]
                upper = jnp.concatenate([real_z, -imag_z], axis=1)
                lower = jnp.concatenate([imag_z, real_z], axis=1)
                left = jnp.concatenate([upper, lower], axis=0)
            else:
                real_z, imag_z = z[:, :sources], z[:, sources:]
                upper = jnp.concatenate([real_z, imag_z], axis=1)
                lower = jnp.concatenate([-imag_z, real_z], axis=1)
                left = jnp.concatenate([upper, lower], axis=0)
            term = matmul(left, u_ref[f, col_ref[f, x]], 1 if turned else 0)
            if x == 0:
                acc_ref[...] = term
            else:
                acc_ref[...] += term
        y_ref[f] = acc_ref[...].astype(jnp.bfloat16).T


def expand(col_map, incoming, u_tiles, cols, turned):
    freq_count = col_map.shape[0]
    rank_block = incoming.shape[-1] if turned else incoming.shape[-2]
    tile_len = u_tiles.shape[-1]
    incoming = incoming.reshape((freq_count, TC) + incoming.shape[1:])
    weights = u_tiles.reshape(freq_count, TC, 2 * rank_block, tile_len)
    return pl.pallas_call(
        lambda *refs: expand_kernel(turned, *refs),
        out_shape=jax.ShapeDtypeStruct((freq_count, tile_len, cols), jnp.bfloat16),
        in_specs=[
            pl.BlockSpec(memory_space=pltpu.SMEM),
            pl.BlockSpec(memory_space=pltpu.VMEM),
            pl.BlockSpec(memory_space=pltpu.VMEM),
        ],
        out_specs=pl.BlockSpec(memory_space=pltpu.VMEM),
        scratch_shapes=[pltpu.VMEM((cols, tile_len), jnp.float32)],
        compiler_params=pltpu.CompilerParams(vmem_limit_bytes=24 * 2**20),
        name="expand",
    )(col_map, incoming, weights)


def split(value):
    high = value.astype(jnp.bfloat16)
    return high, (value - high.astype(jnp.float32)).astype(jnp.bfloat16)


def smoother(sources):
    place = jnp.arange(sources, dtype=jnp.int32)
    row, column = place // SIDE, place % SIDE

    def one(at):
        apart = jnp.abs(at[:, None] - at[None, :])
        return jnp.where(apart == 0, centre_weight, jnp.where(apart == 1, edge_weight, 0.0))

    return jnp.concatenate(split(one(row) * one(column)), axis=0)


def mix_rows(y_ref, cos_g_ref, sin_g_ref, smooth_ref, mix_ref, first, count):
    freq_count, _, blocks, receivers, cols = y_ref.shape
    sources = cols // 2
    many = count * receivers
    for f in range(freq_count):
        if blocks == 1:
            parts = [y_ref[f, first:first + count, 0]]
        else:
            summed = y_ref[f, first:first + count, 0].astype(jnp.float32)
            for k in range(1, blocks):
                summed = summed + y_ref[f, first:first + count, k].astype(jnp.float32)
            parts = split(summed)
        smoothed = None
        for part in parts:
            part = part.reshape(many, cols)
            left = jnp.concatenate([part[:, :sources], part[:, sources:]], axis=0)
            term = matmul(jnp.concatenate([left, left], axis=1), smooth_ref[...])
            smoothed = term if smoothed is None else smoothed + term
        real_y, imag_y = smoothed[:many], smoothed[many:]
        cos_g = cos_g_ref[f, first:first + count].reshape(many, 1)
        sin_g = sin_g_ref[f, first:first + count].reshape(many, 1)
        shape = (count, receivers, sources)
        mix_ref[f, 0, first:first + count] = (cos_g * real_y - sin_g * imag_y).reshape(shape)
        mix_ref[f, 1, first:first + count] = (sin_g * real_y + cos_g * imag_y).reshape(shape)


def gate_kernel(y_ref, cos_g_ref, sin_g_ref, smooth_ref, wave_ref, out_ref, mix_ref):
    rows, receivers, gate_len, sources = out_ref.shape
    freq_count, all_rows = y_ref.shape[:2]
    high = 16

    @pl.when(pl.program_id(0) == 0)
    def _():
        for first in range(0, all_rows, 4):
            mix_rows(y_ref, cos_g_ref, sin_g_ref, smooth_ref, mix_ref, first, 4)

    for i in range(rows):
        row = pl.program_id(0) * rows + i
        for r in range(receivers):
            mixed = [
                [
                    jnp.broadcast_to(mix_ref[f, p, row, r:r + 1], (high, sources)).astype(
                        jnp.bfloat16
                    )
                    for p in range(2)
                ]
                for f in range(freq_count)
            ]
            for top in range(0, gate_len, high):
                down = slice(top, top + high)
                terms = [
                    wave_ref[f, 0, down] * mixed[f][0] - wave_ref[f, 1, down] * mixed[f][1]
                    for f in range(freq_count)
                ]
                total = terms[0]
                if freq_count > 1:
                    total = sum(term.astype(jnp.float32) for term in terms)
                out_ref[i, r, down] = total.astype(out_ref.dtype)


def gate(arrived, cos_g, sin_g, smooth, wave, step):
    freq_count, rows, _, receivers, cols = arrived.shape
    sources = cols // 2
    gate_len = wave.shape[2]
    return pl.pallas_call(
        gate_kernel,
        out_shape=jax.ShapeDtypeStruct((rows, receivers, gate_len, sources), jnp.bfloat16),
        grid=(rows // step,),
        in_specs=[pl.BlockSpec(memory_space=pltpu.VMEM)] * 5,
        out_specs=pl.BlockSpec((step, receivers, gate_len, sources), lambda i: (i, 0, 0, 0)),
        scratch_shapes=[pltpu.VMEM((freq_count, 2, rows, receivers, sources), jnp.float32)],
        compiler_params=pltpu.CompilerParams(vmem_limit_bytes=32 * 2**20),
        name="gate",
    )(arrived, cos_g, sin_g, smooth, wave)


def waves(times, bins):
    phases = bins.reshape((-1,) + (1,) * times.ndim) * times[None] % NT
    angles = phases.astype(jnp.float32) * (2.0 * math.pi / NT)
    return jnp.cos(angles), jnp.sin(angles)


def gate_waves(bins, lanes):
    both = jnp.stack(waves(jnp.arange(GT, dtype=jnp.int32), bins), axis=1).astype(jnp.bfloat16)
    return jnp.broadcast_to(both[..., None], both.shape + (lanes,))


def on_device(src_slots, v_tiles, u_tiles, ranks, col_map, gate_start):
    devices = lax.axis_size("tile")
    freq_count = devices // TC
    blocks_per = devices // TR
    rank_block = RMAX // blocks_per
    turned = rank_block == RMAX
    cols = src_slots.shape[-1]
    tile_len = v_tiles.shape[2]
    receivers = tile_len // devices
    freq_ids = jnp.arange(freq_count, dtype=jnp.int32)

    outgoing = project(ranks, col_map, v_tiles, src_slots, 4, turned)
    if not turned:
        outgoing = outgoing.reshape(devices, rank_block, cols)
    incoming = lax.all_to_all(outgoing, "tile", split_axis=0, concat_axis=0, tiled=True)
    partial_value = expand(col_map, incoming, u_tiles, cols, turned)
    spread = partial_value.reshape(freq_count, devices, receivers, cols)
    arrived = lax.all_to_all(spread, "tile", split_axis=1, concat_axis=1, tiled=True)
    arrived = arrived.reshape(freq_count, TR, blocks_per, receivers, cols)

    bins = 4 + freq_ids * (NT // (2 * freq_count))
    scale = 2.0 / math.sqrt(freq_count)
    cos_g, sin_g = waves(gate_start, bins)
    cos_g, sin_g = scale * cos_g[..., None], scale * sin_g[..., None]
    wave = gate_waves(bins, cols // 2)
    return gate(arrived, cos_g, sin_g, smoother(cols // 2), wave, 2)


def solution(mesh):
    placed = (
        P(("parts", "tile"), None, None),
        P(("parts", "tile"), None, None, None),
        P(("parts", "tile"), None, None, None),
        P("parts", None, None),
        P("parts", None),
        P("parts", "tile"),
    )
    return jax.shard_map(
        on_device,
        mesh=mesh,
        in_specs=placed,
        out_specs=P("parts", "tile", None, None),
        check_vma=False,
    )
```

time: 265 us -> 91.9 us (0.35)
  local copies, waits for them, and re-layouts: 93 us -> 0.44 us
  other arithmetic: 90.3 us -> 0.38 us
  Pallas kernels: 0 us -> 17.3 us
  matrix products: 8.97 us -> 0 us
    slice x2 -> x0, local copies, waits for them, and re-layouts: 91.8 us -> none  [the longest x1 45.9 us: smooth_grid(): before = jnp.concatenate([zeros_one, signal[..., :-1]], axis=-1)]
    convert_element_type x2 -> x1, other arithmetic: 38.8 us -> 0.23 us  [split(): high = value.astype(jnp.bfloat16)]
    add x1 -> x0, other arithmetic: 33.8 us -> none  [smooth_grid(): across = centre_weight * signal + edge_weight * (before + after)]
    pallas_call x0 -> x3, Pallas kernels: none -> 17.3 us  [the longest x1 7.44 us: gate(): pl.pallas_call(gate_kernel, out_shape=jax.ShapeDtypeStruct((rows, receive...]
    mul x1, other arithmetic: 11.7 us -> 0.06 us  [on_device(): cos_g, sin_g = (scale * cos_g[..., None], scale * sin_g[..., None])]
    dot_general x3 -> x0, matrix products: 8.97 us -> none  [the longest x1 4.58 us: on_device(): jnp.einsum('ibr,bs->irs', v_tiles[0], src_slots[0], preferred_element_typ...]
  transfers between devices with their start and end apart: 1 -> 1, of which waited for: 1 -> 1; matrix products, arithmetic and copies ran while one was open for 0% -> 1% of each run, Pallas kernels for 0% -> 0%
where the time goes in v2:
time: 91.9 us; the launch traced here: 91.6 us
  blocking collectives  54.8 us (60%)
  Pallas kernels  17.3 us (19%)
  waiting for transfers between devices  13.5 us (15%)
  starting transfers between devices  5.14 us (6%)
    all_to_all x1, blocking collectives, on_device(): lax.all_to_all(outgoing, 'tile', split_axis=0, concat_axis=0, tiled=True)  54.8 us
    all_to_all x1, waiting for transfers between devices, on_device(): lax.all_to_all(spread, 'tile', split_axis=1, concat_axis=1, tiled=True)  13.5 us
    pallas_call x1, Pallas kernels, gate(): pl.pallas_call(gate_kernel, out_shape=jax.ShapeDtypeStruct((rows, receive...  7.44 us
    pallas_call x1, Pallas kernels, project(): pl.pallas_call(lambda *refs: project_kernel(turned, *refs), out_shape=jax...  6.09 us
    all_to_all x1, starting transfers between devices, on_device(): lax.all_to_all(spread, 'tile', split_axis=1, concat_axis=1, tiled=True)  5.14 us
    pallas_call x1, Pallas kernels, expand(): pl.pallas_call(lambda *refs: expand_kernel(turned, *refs), out_shape=jax....  3.74 us
  transfers between devices with their start and end apart: 1, of which 1 were waited for; matrix products, arithmetic and copies ran while one was open for 1% of the time, Pallas kernels for 0%

profile of v2, /device:TPU:0, one launch (start us, length us, event | category | flops | bytes accessed | tf_op | source)
XLA Modules:
  0.0 91.6 jit_solution(470757973230871958)
XLA Ops:
  0.0 0.0 copy-start.1
  0.0 6.1 %project.1 = bf16[16,512,128]{2,1,0:T(8,128)(2,1)} custom-call(s32[1,16,16]{2,1,0:T(8,128)} %refs_0_.2, s32[1,16]{1,0:T(1,128)} %refs_0_.3, bf16[1,16,512,256]{3,2,1,0:T(8,128)(2,1)} %refs_2_.2, bf16[1,512,512]{2,1,0:T(8,128)(2,1)} %refs_3_.1), custom_call_target="tpu_custom_call" | custom-call | tf_op jit(solution)/shard_map/project/pallas_call | solution.py:63
  6.1 0.0 copy-start
  6.1 54.8 %all_to_all.10 = bf16[16,512,128]{2,1,0:T(8,128)(2,1)S(1)} all-to-all(bf16[16,512,128]{2,1,0:T(8,128)(2,1)} %project.1), channel_id=1, replica_groups=mesh['parts'=2,'tile'=16] {'tile'}, dimensions={0} | all-to-all | bytes 4194304 | tf_op jit(solution)/shard_map/all_to_all | solution.py:241
  60.9 0.0 copy-start.2
  60.9 0.0 copy-done.1
  60.9 0.0 copy-done
  60.9 3.7 %expand.1 = bf16[1,512,512]{2,1,0:T(8,128)(2,1)} custom-call(s32[1,16]{1,0:T(1,128)S(1)} %copy-done.1, bf16[1,16,512,128]{3,2,1,0:T(8,128)(2,1)S(1)} %bitcast.9, bf16[1,16,256,512]{3,2,1,0:T(8,128)(2,1)S(1)} %copy-done), custom_call_target="tpu_custom_call" | custom-call | tf_op jit(solution)/shard_map/expand/pallas_call | solution.py:109
  64.7 5.1 %all-to-all-start.1 = ((bf16[1,16,32,512]{3,2,0,1:T(8,128)(2,1)}), bf16[1,16,32,512]{3,2,0,1:T(8,128)(2,1)S(1)}, u32[]{:S(2)}, u32[]{:S(2)}) async-start(bf16[1,16,32,512]{3,2,0,1:T(8,128)(2,1)} %bitcast.2), calls=%async_computation.1 | async-start | bytes 1048576 | tf_op jit(solution)/shard_map/all_to_all | solution.py:244
  69.8 0.0 copy-done.2
  69.8 0.1 multiply_bitcast_fusion
  69.9 0.2 copy.13.sin_g_ref
  70.1 0.2 copy.12.cos_g_ref
  70.2 0.1 sine_convert_fusion
  70.3 0.2 fusion.4
  70.6 13.5 %all-to-all-done.1 = bf16[1,16,32,512]{3,2,0,1:T(8,128)(2,1)S(1)} async-done(((bf16[1,16,32,512]{3,2,0,1:T(8,128)(2,1)}), bf16[1,16,32,512]{3,2,0,1:T(8,128)(2,1)S(1)}, u32[]{:S(2)}, u32[]{:S(2)}) %all-to-all-start.1) | async-done | bytes 524320 | tf_op jit(solution)/shard_map/all_to_all | solution.py:244
  84.1 0.1 broadcast_in_dim.32.wave_ref
  84.2 7.4 %gate.1 = bf16[16,32,64,256]{3,2,1,0:T(8,128)(2,1)} custom-call(bf16[1,16,1,32,512]{4,3,2,1,0:T(8,128)(2,1)S(1)} %bitcast.10, f32[1,16,32,1]{3,2,1,0:T(8,128)S(1)} %copy.12.cos_g_ref, f32[1,16,32,1]{3,2,1,0:T(8,128)S(1)} %copy.13.sin_g_ref, bf16[512,256]{1,0:T(8,128)(2,1)S(1)} %pad_maximum_fusion.smooth_ref, ...), custom_call_target="tpu_custom_call" | custom-call | tf_op jit(solution)/shard_map/gate/pallas_call | solution.py:204
  (3 shorter events, 0.0 us)
Async XLA Ops:
  0.0 60.9 %copy-start.1 = (s32[1,16]{1,0:T(1,128)S(1)}, s32[1,16]{1,0:T(1,128)}, u32[]{:S(2)}) copy-start(s32[1,16]{1,0:T(1,128)} %refs_0_.3) | copy-start | bytes 196
  6.1 54.8 %copy-start = (bf16[1,16,256,512]{3,2,1,0:T(8,128)(2,1)S(1)}, bf16[1,16,256,512]{3,2,1,0:T(8,128)(2,1)}, u32[]{:S(2)}) copy-start(bf16[1,16,256,512]{3,2,1,0:T(8,128)(2,1)} %refs_2_.3) | copy-start | bytes 12582916
  60.9 8.9 %copy-start.2 = (s32[16,32]{1,0:T(8,128)S(1)}, s32[16,32]{1,0:T(8,128)}, u32[]{:S(2)}) copy-start(s32[16,32]{1,0:T(8,128)} %param.11) | copy-start | bytes 6148
  64.7 19.4 %all-to-all-start.1 = ((bf16[1,16,32,512]{3,2,0,1:T(8,128)(2,1)}), bf16[1,16,32,512]{3,2,0,1:T(8,128)(2,1)S(1)}, u32[]{:S(2)}, u32[]{:S(2)}) async-start(bf16[1,16,32,512]{3,2,0,1:T(8,128)(2,1)} %bitcast.2), calls=%async_computation.1 | async-start | bytes 1048576 | tf_op jit(solution)/shard_map/all_to_all | solution.py:244

commit v3 on v2

--- a/solution.py
+++ b/solution.py
@@ -1,3 +1,4 @@
+import functools
 import math
 
 import jax
@@ -7,12 +8,16 @@
 from jax.experimental.pallas import tpu as pltpu
 from jax.sharding import PartitionSpec as P
 
+
 TC = 16
 TR = 16
 RMAX = 128
 SIDE = 16
 NT = 1024
 GT = 64
+sends = (2, 6, 8)
+takes = (8, 6, 2)
+
 
 edge_weight = 0.15
 centre_weight = 0.7
@@ -119,6 +124,180 @@
         compiler_params=pltpu.CompilerParams(vmem_limit_bytes=24 * 2**20),
         name="expand",
     )(col_map, incoming, weights)
+
+
+def far_first(devices):
+    return sorted(range(1, devices), key=lambda k: (-(k >> 2), k)) + [0]
+
+
+def send_first_kernel(ids, rank_hbm, col_hbm, v_hbm, x_hbm, *refs):
+    count = len(ids)
+    z_refs = refs[:count]
+    left_ref, x_ref, tile_ref, rank_ref, col_ref, sems = refs[count:]
+    device = lax.axis_index("tile")
+    rows = [jnp.bitwise_xor(device, k) for k in ids]
+    copies = [
+        pltpu.make_async_copy(x_hbm.at[0], x_ref, sems.at[count]),
+        pltpu.make_async_copy(rank_hbm.at[0], rank_ref, sems.at[count + 1]),
+        pltpu.make_async_copy(col_hbm, col_ref, sems.at[count + 2]),
+    ]
+    for n, row in enumerate(rows):
+        copies.append(pltpu.make_async_copy(v_hbm.at[0, row], tile_ref.at[n], sems.at[n]))
+    for copy in copies:
+        copy.start()
+    copies[0].wait()
+    build_left(x_ref[...], left_ref)
+    for copy in copies[1:]:
+        copy.wait()
+    column = col_ref[0, device]
+    for n in range(0, count, 2):
+        tiles = [tile_ref[n], tile_ref[n + 1]]
+        ranks = [rank_ref[rows[n], column], rank_ref[rows[n + 1], column]]
+        z_refs[n][...], z_refs[n + 1][...] = project_two(left_ref, tiles, ranks)
+
+
+def build_left(x, left_ref):
+    tile_len, cols = x.shape
+    sources = cols // 2
+    real_x = x[:, :sources].T
+    imag_x = x[:, sources:].T
+    left_ref[:sources, :tile_len] = real_x
+    left_ref[:sources, tile_len:] = -imag_x
+    left_ref[sources:, :tile_len] = imag_x
+    left_ref[sources:, tile_len:] = real_x
+
+
+def send_kernel(ids, rank_ref, col_ref, v_ref, x_ref, *refs):
+    z_refs, left_ref = refs[:-1], refs[-1]
+    build_left(x_ref[0], left_ref)
+    device = lax.axis_index("tile")
+    column = col_ref[0, device]
+    rows = [jnp.bitwise_xor(device, k) for k in ids]
+    for n in range(0, len(ids), 2):
+        tiles = [v_ref[0, rows[n]], v_ref[0, rows[n + 1]]]
+        ranks = [rank_ref[0, rows[n], column], rank_ref[0, rows[n + 1], column]]
+        z_refs[n][...], z_refs[n + 1][...] = project_two(left_ref, tiles, ranks)
+
+
+def project_two(left_ref, tiles, ranks):
+    lane = lax.broadcasted_iota(jnp.int32, (1, 2 * RMAX), 1)
+    one, two = tiles
+    real_v = jnp.concatenate([one[:, :RMAX], two[:, :RMAX]], axis=1)
+    imag_v = jnp.concatenate([one[:, RMAX:], two[:, RMAX:]], axis=1)
+    both = matmul(left_ref[...], jnp.concatenate([real_v, imag_v], axis=0))
+    live = (lane < ranks[0]) | ((lane >= RMAX) & (lane < ranks[1] + RMAX))
+    both = jnp.where(live, both, 0.0).astype(jnp.bfloat16)
+    return both[:, :RMAX], both[:, RMAX:]
+
+
+def send_tiles(ids, ranks, col_map, v_tiles, src_slots, first):
+    tile_len, wide = v_tiles.shape[2:]
+    cols = src_slots.shape[-1]
+    count = len(ids)
+    vmem, smem, hbm = (
+        pl.BlockSpec(memory_space=m) for m in (pltpu.VMEM, pltpu.SMEM, pltpu.HBM)
+    )
+    left = pltpu.VMEM((cols, 2 * tile_len), jnp.bfloat16)
+    scratch = [
+        left,
+        pltpu.VMEM((tile_len, cols), jnp.bfloat16),
+        pltpu.VMEM((count, tile_len, wide), jnp.bfloat16),
+        pltpu.SMEM(ranks.shape[1:], jnp.int32),
+        pltpu.SMEM(col_map.shape, jnp.int32),
+        pltpu.SemaphoreType.DMA((count + 3,)),
+    ]
+    return pl.pallas_call(
+        functools.partial(send_first_kernel if first else send_kernel, ids),
+        out_shape=[jax.ShapeDtypeStruct((cols, RMAX), jnp.bfloat16) for _ in ids],
+        in_specs=[hbm] * 4 if first else [smem, smem, vmem, vmem],
+        out_specs=[vmem] * count,
+        scratch_shapes=scratch if first else [left],
+        compiler_params=pltpu.CompilerParams(
+            vmem_limit_bytes=(60 if first else 12) * 2**20
+        ),
+        cost_estimate=pl.CostEstimate(
+            flops=2 * count * cols * 2 * tile_len * RMAX,
+            bytes_accessed=count * tile_len * wide * 2,
+            transcendentals=0,
+        ),
+        name="send_first" if first else "send_tiles",
+    )(ranks, col_map, v_tiles, src_slots)
+
+
+def add_kernel(ids, first, last, col_ref, u_ref, *refs):
+    count = len(ids)
+    z_refs, out_ref = refs[:count], refs[count if first else count + 1]
+    total_ref = refs[-1]
+    sources = z_refs[0].shape[0] // 2
+    device = lax.axis_index("tile")
+    for n, k in enumerate(ids):
+        z = z_refs[n][...]
+        real_z, imag_z = z[:sources], z[sources:]
+        upper = jnp.concatenate([real_z, -imag_z], axis=1)
+        lower = jnp.concatenate([imag_z, real_z], axis=1)
+        left = jnp.concatenate([upper, lower], axis=0)
+        term = matmul(left, u_ref[0, col_ref[0, jnp.bitwise_xor(device, k)]])
+        if n == 0:
+            total_ref[...] = term if first else refs[count][...] + term
+        else:
+            total_ref[...] += term
+    if last:
+        out_ref[0] = total_ref[...].astype(jnp.bfloat16).T
+    else:
+        out_ref[...] = total_ref[...]
+
+
+def add_tiles(ids, tiles, col_map, u_tiles, total=None, last=False):
+    first = total is None
+    cols = tiles[0].shape[0]
+    tile_len = u_tiles.shape[-1]
+    vmem, smem = (pl.BlockSpec(memory_space=m) for m in (pltpu.VMEM, pltpu.SMEM))
+    operands = [col_map, u_tiles, *tiles] + ([] if first else [total])
+    shape = (
+        jax.ShapeDtypeStruct((1, tile_len, cols), jnp.bfloat16)
+        if last
+        else jax.ShapeDtypeStruct((cols, tile_len), jnp.float32)
+    )
+    flops = 2 * len(ids) * cols * 2 * RMAX * tile_len
+    return pl.pallas_call(
+        lambda *refs: add_kernel(ids, first, last, *refs),
+        out_shape=shape,
+        in_specs=[smem] + [vmem] * (len(operands) - 1),
+        out_specs=vmem,
+        scratch_shapes=[pltpu.VMEM((cols, tile_len), jnp.float32)],
+        compiler_params=pltpu.CompilerParams(vmem_limit_bytes=12 * 2**20),
+        cost_estimate=pl.CostEstimate(
+            flops=flops, bytes_accessed=len(ids) * cols * RMAX * 2, transcendentals=0
+        ),
+        name="add_tiles",
+    )(*operands)
+
+
+def far_last(devices):
+    half = devices // 2
+    return list(range(half)) + [k for k in far_first(devices) if k >= half]
+
+
+def exchange(ranks, col_map, v_tiles, src_slots, u_tiles):
+    devices = lax.axis_size("tile")
+    arrived, at = {}, 0
+    for group, count in enumerate(sends):
+        ids = far_first(devices)[at:at + count]
+        tiles = send_tiles(ids, ranks, col_map, v_tiles, src_slots, group == 0)
+        for k, tile in zip(ids, tiles):
+            arrived[k] = tile
+            if k:
+                pairs = [(d, d ^ k) for d in range(devices)]
+                arrived[k] = lax.ppermute(tile, "tile", pairs)
+        at += count
+    total, at = None, 0
+    for count in takes:
+        ids = far_last(devices)[at:at + count]
+        at += count
+        total = add_tiles(
+            ids, [arrived[k] for k in ids], col_map, u_tiles, total, at == devices
+        )
+    return total
 
 
 def split(value):
@@ -168,9 +347,10 @@
     freq_count, all_rows = y_ref.shape[:2]
     high = 16
 
-    @pl.when(pl.program_id(0) == 0)
-    def _():
-        for first in range(0, all_rows, 4):
+    for first in range(0, all_rows, 4):
+
+        @pl.when(pl.program_id(0) * rows == first)
+        def _():
             mix_rows(y_ref, cos_g_ref, sin_g_ref, smooth_ref, mix_ref, first, 4)
 
     for i in range(rows):
@@ -235,11 +415,13 @@
     receivers = tile_len // devices
     freq_ids = jnp.arange(freq_count, dtype=jnp.int32)
 
-    outgoing = project(ranks, col_map, v_tiles, src_slots, 4, turned)
-    if not turned:
+    if turned:
+        partial_value = exchange(ranks, col_map, v_tiles, src_slots, u_tiles)
+    else:
+        outgoing = project(ranks, col_map, v_tiles, src_slots, 4, turned)
         outgoing = outgoing.reshape(devices, rank_block, cols)
-    incoming = lax.all_to_all(outgoing, "tile", split_axis=0, concat_axis=0, tiled=True)
-    partial_value = expand(col_map, incoming, u_tiles, cols, turned)
+        incoming = lax.all_to_all(outgoing, "tile", split_axis=0, concat_axis=0, tiled=True)
+        partial_value = expand(col_map, incoming, u_tiles, cols, turned)
     spread = partial_value.reshape(freq_count, devices, receivers, cols)
     arrived = lax.all_to_all(spread, "tile", split_axis=1, concat_axis=1, tiled=True)
     arrived = arrived.reshape(freq_count, TR, blocks_per, receivers, cols)
@@ -249,7 +431,7 @@
     cos_g, sin_g = waves(gate_start, bins)
     cos_g, sin_g = scale * cos_g[..., None], scale * sin_g[..., None]
     wave = gate_waves(bins, cols // 2)
-    return gate(arrived, cos_g, sin_g, smoother(cols // 2), wave, 2)
+    return gate(arrived, cos_g, sin_g, smoother(cols // 2), wave, 4)
 
 
 def solution(mesh):

time: 91.9 us -> 88.4 us (0.962)
  blocking collectives: 54.8 us -> 0 us
  starting transfers between devices: 5.14 us -> 31.7 us
  waiting for transfers between devices: 13.5 us -> 35.1 us
  local copies, waits for them, and re-layouts: 0.44 us -> 2.64 us
    all_to_all x1 -> x0, blocking collectives: 54.8 us -> none  [on_device(): lax.all_to_all(outgoing, 'tile', split_axis=0, concat_axis=0, tiled=True)]
    ppermute x0 -> x15, starting transfers between devices: none -> 27.2 us  [exchange(): arrived[k] = lax.ppermute(tile, 'tile', pairs)]
    ppermute x0 -> x15, waiting for transfers between devices: none -> 21.6 us  [exchange(): arrived[k] = lax.ppermute(tile, 'tile', pairs)]
    unnamed x6 -> x12, local copies, waits for them, and re-layouts: 0.01 us -> 2.2 us
    pallas_call x2 -> x6, Pallas kernels: 9.83 us -> 11.3 us  [the longest x3 6.12 us: send_tiles(): pl.pallas_call(functools.partial(send_first_kernel if first else send_ker...]
  transfers between devices with their start and end apart: 1 -> 16, of which waited for: 1 -> 6; matrix products, arithmetic and copies ran while one was open for 1% -> 1% of each run, Pallas kernels for 0% -> 8%
where the time goes in v3:
time: 88.4 us; the launch traced here: 88.1 us
  waiting for transfers between devices  35.1 us (40%)
  starting transfers between devices  31.7 us (36%)
  Pallas kernels  18.2 us (21%)
  local copies, waits for them, and re-layouts  2.64 us (3%)
    ppermute x15, starting transfers between devices, exchange(): arrived[k] = lax.ppermute(tile, 'tile', pairs)  27.2 us
    ppermute x15, waiting for transfers between devices, exchange(): arrived[k] = lax.ppermute(tile, 'tile', pairs)  21.6 us
    all_to_all x1, waiting for transfers between devices, on_device(): lax.all_to_all(spread, 'tile', split_axis=1, concat_axis=1, tiled=True)  13.5 us
    pallas_call x1, Pallas kernels, gate(): pl.pallas_call(gate_kernel, out_shape=jax.ShapeDtypeStruct((rows, receive...  6.86 us
    pallas_call x3, Pallas kernels, send_tiles(): pl.pallas_call(functools.partial(send_first_kernel if first else send_ker...  6.12 us
    pallas_call x3, Pallas kernels, add_tiles(): pl.pallas_call(lambda *refs: add_kernel(ids, first, last, *refs), out_sha...  5.18 us
    all_to_all x1, starting transfers between devices, on_device(): lax.all_to_all(spread, 'tile', split_axis=1, concat_axis=1, tiled=True)  4.5 us
    unnamed x12, local copies, waits for them, and re-layouts  2.2 us
  transfers between devices with their start and end apart: 16, of which 6 were waited for; matrix products, arithmetic and copies ran while one was open for 1% of the time, Pallas kernels for 8%

profile of v3, /device:TPU:0, one launch (start us, length us, event | category | flops | bytes accessed | tf_op | source)
XLA Modules:
  0.0 88.1 jit_solution(14256911241188375884)
XLA Ops:
  0.0 2.5 %send_first.1 = (bf16[512,128]{1,0:T(8,128)(2,1)}, bf16[512,128]{1,0:T(8,128)(2,1)}) custom-call(s32[1,16,16]{2,1,0:T(8,128)} %rank_ref.3, s32[1,16]{1,0:T(1,128)} %refs_0_.5, bf16[1,16,512,256]{3,2,1,0:T(8,128)(2,1)} %v_ref.3, bf16[1,512,512]{2,1,0:T(8,128)(2,1)} %x_ref.3), custom_call_target="tpu_custom_call" | custom-call | flops 268435456 | bytes 524288 | tf_op jit(solution)/shard_map/send_first/pallas_call | solution.py:209
  2.5 5.1 %collective-permute-start.2 = (bf16[512,128]{1,0:T(8,128)(2,1)}, bf16[512,128]{1,0:T(8,128)(2,1)S(1)}, u32[]{:S(2)}, u32[]{:S(2)}) collective-permute-start(bf16[512,128]{1,0:T(8,128)(2,1)} %get-tuple-element.23), channel_id=1, source_target_pairs={{0,12},{1,13},{2,14},{3,15},{4,8},{5,9},{6,10},{7,11},{8,4},{9,5},... | collective-permute-start | bytes 393224 | tf_op jit(solution)/shard_map/ppermute | solution.py:291
  7.7 2.2 %copy-done = bf16[1,16,512,256]{3,2,1,0:T(8,128)(2,1)S(1)} copy-done((bf16[1,16,512,256]{3,2,1,0:T(8,128)(2,1)S(1)}, bf16[1,16,512,256]{3,2,1,0:T(8,128)(2,1)}, u32[]{:S(2)}) %copy-start) | copy-done | bytes 4194328
  9.9 1.7 %send_tiles.2 = (bf16[512,128]{1,0:T(8,128)(2,1)S(1)}, bf16[512,128]{1,0:T(8,128)(2,1)S(1)}, bf16[512,128]{1,0:T(8,128)(2,1)S(1)}, bf16[512,128]{1,0:T(8,128)(2,...) custom-call(s32[1,16,16]{2,1,0:T(8,128)S(1)} %copy-done.3, s32[1,16]{1,0:T(1,128)S(1)} %copy-done.4, ...), custom_call_target="tpu_custom_call" | custom-call | flops 805306368 | bytes 1572864 | tf_op jit(solution)/shard_map/send_tiles/pallas_call | solution.py:209
  11.6 4.0 %collective-permute-start.4 = (bf16[512,128]{1,0:T(8,128)(2,1)S(1)}, bf16[512,128]{1,0:T(8,128)(2,1)S(1)}, u32[]{:S(2)}, u32[]{:S(2)}) collective-permute-start(bf16[512,128]{1,0:T(8,128)(2,1)S(1)} %get-tuple-element.25), channel_id=1, source_target_pairs={{0,14},{1,15},{2,12},{3,13},{4,10},{5,11},{6,8},{7,9},{8,6},{9,7},... | collective-permute-start | bytes 393224 | tf_op jit(solution)/shard_map/ppermute | solution.py:291
  15.5 1.9 %send_tiles.3 = (bf16[512,128]{1,0:T(8,128)(2,1)S(1)}, bf16[512,128]{1,0:T(8,128)(2,1)S(1)}, bf16[512,128]{1,0:T(8,128)(2,1)S(1)}, bf16[512,128]{1,0:T(8,128)(2,...) custom-call(s32[1,16,16]{2,1,0:T(8,128)S(1)} %copy-done.3, ...), custom_call_target="tpu_custom_call" | custom-call | flops 1073741824 | bytes 2097152 | tf_op jit(solution)/shard_map/send_tiles/pallas_call | solution.py:209
  18.8 0.9 %collective-permute-start.10 = (bf16[512,128]{1,0:T(8,128)(2,1)S(1)}, bf16[512,128]{1,0:T(8,128)(2,1)S(1)}, u32[]{:S(2)}, u32[]{:S(2)}) collective-permute-start(bf16[512,128]{1,0:T(8,128)(2,1)S(1)} %get-tuple-element.32), channel_id=1, source_target_pairs={{0,3},{1,2},{2,1},{3,0},{4,7},{5,6},{6,5},{7,4},{8,11},{9,10},{10,... | collective-permute-start | bytes 393224 | tf_op jit(solution)/shard_map/ppermute | solution.py:291
  19.7 3.0 %collective-permute-start.11 = (bf16[512,128]{1,0:T(8,128)(2,1)S(1)}, bf16[512,128]{1,0:T(8,128)(2,1)S(1)}, u32[]{:S(2)}, u32[]{:S(2)}) collective-permute-start(bf16[512,128]{1,0:T(8,128)(2,1)S(1)} %get-tuple-element.33), channel_id=1, source_target_pairs={{0,4},{1,5},{2,6},{3,7},{4,0},{5,1},{6,2},{7,3},{8,12},{9,13},{10,... | collective-permute-start | bytes 393224 | tf_op jit(solution)/shard_map/ppermute | solution.py:291
  22.6 2.2 %collective-permute-start.12 = (bf16[512,128]{1,0:T(8,128)(2,1)S(1)}, bf16[512,128]{1,0:T(8,128)(2,1)S(1)}, u32[]{:S(2)}, u32[]{:S(2)}) collective-permute-start(bf16[512,128]{1,0:T(8,128)(2,1)S(1)} %get-tuple-element.34), channel_id=1, source_target_pairs={{0,5},{1,4},{2,7},{3,6},{4,1},{5,0},{6,3},{7,2},{8,13},{9,12},{10,... | collective-permute-start | bytes 393224 | tf_op jit(solution)/shard_map/ppermute | solution.py:291
  24.9 1.3 %collective-permute-start.13 = (bf16[512,128]{1,0:T(8,128)(2,1)S(1)}, bf16[512,128]{1,0:T(8,128)(2,1)S(1)}, u32[]{:S(2)}, u32[]{:S(2)}) collective-permute-start(bf16[512,128]{1,0:T(8,128)(2,1)S(1)} %get-tuple-element.35), channel_id=1, source_target_pairs={{0,6},{1,7},{2,4},{3,5},{4,2},{5,3},{6,0},{7,1},{8,14},{9,15},{10,... | collective-permute-start | bytes 393224 | tf_op jit(solution)/shard_map/ppermute | solution.py:291
  26.1 2.4 %collective-permute-start.14 = (bf16[512,128]{1,0:T(8,128)(2,1)S(1)}, bf16[512,128]{1,0:T(8,128)(2,1)S(1)}, u32[]{:S(2)}, u32[]{:S(2)}) collective-permute-start(bf16[512,128]{1,0:T(8,128)(2,1)S(1)} %get-tuple-element.36), channel_id=1, source_target_pairs={{0,7},{1,6},{2,5},{3,4},{4,3},{5,2},{6,1},{7,0},{8,15},{9,14},{10,... | collective-permute-start | bytes 393224 | tf_op jit(solution)/shard_map/ppermute | solution.py:291
  28.6 1.2 %collective-permute-start.5 = (bf16[512,128]{1,0:T(8,128)(2,1)S(1)}, bf16[512,128]{1,0:T(8,128)(2,1)S(1)}, u32[]{:S(2)}, u32[]{:S(2)}) collective-permute-start(bf16[512,128]{1,0:T(8,128)(2,1)S(1)} %get-tuple-element.26), channel_id=1, source_target_pairs={{0,15},{1,14},{2,13},{3,12},{4,11},{5,10},{6,9},{7,8},{8,7},{9,6},... | collective-permute-start | bytes 393224 | tf_op jit(solution)/shard_map/ppermute | solution.py:291
  30.2 3.1 %collective-permute-start.7 = (bf16[512,128]{1,0:T(8,128)(2,1)S(1)}, bf16[512,128]{1,0:T(8,128)(2,1)S(1)}, u32[]{:S(2)}, u32[]{:S(2)}) collective-permute-start(bf16[512,128]{1,0:T(8,128)(2,1)S(1)} %get-tuple-element.28), channel_id=1, source_target_pairs={{0,9},{1,8},{2,11},{3,10},{4,13},{5,12},{6,15},{7,14},{8,1},{9,0},... | collective-permute-start | bytes 393224 | tf_op jit(solution)/shard_map/ppermute | solution.py:291
  33.5 2.2 %collective-permute-start = (bf16[512,128]{1,0:T(8,128)(2,1)S(1)}, bf16[512,128]{1,0:T(8,128)(2,1)S(1)}, u32[]{:S(2)}, u32[]{:S(2)}) collective-permute-start(bf16[512,128]{1,0:T(8,128)(2,1)S(1)} %get-tuple-element.21), channel_id=1, source_target_pairs={{0,10},{1,11},{2,8},{3,9},{4,14},{5,15},{6,12},{7,13},{8,2},{9,3},... | collective-permute-start | bytes 393224 | tf_op jit(solution)/shard_map/ppermute | solution.py:291
  35.8 8.5 %collective-permute-done.14.refs_9_ = bf16[512,128]{1,0:T(8,128)(2,1)S(1)} collective-permute-done((bf16[512,128]{1,0:T(8,128)(2,1)S(1)}, bf16[512,128]{1,0:T(8,128)(2,1)S(1)}, u32[]{:S(2)}, u32[]{:S(2)}) %collective-permute-start.14) | collective-permute-done | bytes 131104 | tf_op jit(solution)/shard_map/ppermute | solution.py:291
  44.3 1.8 %add_tiles.3.refs_8_ = f32[512,512]{1,0:T(8,128)S(1)} custom-call(s32[1,16]{1,0:T(1,128)S(1)} %copy-done.4, bf16[1,16,256,512]{3,2,1,0:T(8,128)(2,1)S(1)} %copy-done.1, bf16[512,128]{1,0:T(8,128)(2,1)S(1)} %get-tuple-element.29.refs_2_, bf16[512,128]{1,0:T(8,128)(2,1)S(1)} %collective-permute-done.8.refs_3_, ...), custom_call_target="tpu_custom_call" | custom-call | flops 1073741824 | bytes 1048576 | tf_op jit(solution)/shard_map/add_tiles/pallas_call | solution.py:262
  46.1 8.6 %collective-permute-done.7.refs_7_ = bf16[512,128]{1,0:T(8,128)(2,1)S(1)} collective-permute-done((bf16[512,128]{1,0:T(8,128)(2,1)S(1)}, bf16[512,128]{1,0:T(8,128)(2,1)S(1)}, u32[]{:S(2)}, u32[]{:S(2)}) %collective-permute-start.7) | collective-permute-done | bytes 131104 | tf_op jit(solution)/shard_map/ppermute | solution.py:291
  54.7 1.5 %add_tiles.4.refs_4_ = f32[512,512]{1,0:T(8,128)S(1)} custom-call(s32[1,16]{1,0:T(1,128)S(1)} %copy-done.4, bf16[1,16,256,512]{3,2,1,0:T(8,128)(2,1)S(1)} %copy-done.1, bf16[512,128]{1,0:T(8,128)(2,1)S(1)} %collective-permute-done.2.refs_2_, bf16[512,128]{1,0:T(8,128)(2,1)S(1)} %collective-permute-done.3.refs_3_, ...), custom_call_target="tpu_custom_call" | custom-call | flops 805306368 | bytes 786432 | tf_op jit(solution)/shard_map/add_tiles/pallas_call | solution.py:262
  56.2 1.2 %collective-permute-done.refs_2_ = bf16[512,128]{1,0:T(8,128)(2,1)S(1)} collective-permute-done((bf16[512,128]{1,0:T(8,128)(2,1)S(1)}, bf16[512,128]{1,0:T(8,128)(2,1)S(1)}, u32[]{:S(2)}, u32[]{:S(2)}) %collective-permute-start) | collective-permute-done | bytes 131104 | tf_op jit(solution)/shard_map/ppermute | solution.py:291
  57.4 3.2 %collective-permute-done.1.refs_3_ = bf16[512,128]{1,0:T(8,128)(2,1)S(1)} collective-permute-done((bf16[512,128]{1,0:T(8,128)(2,1)S(1)}, bf16[512,128]{1,0:T(8,128)(2,1)S(1)}, u32[]{:S(2)}, u32[]{:S(2)}) %collective-permute-start.1) | collective-permute-done | bytes 131104 | tf_op jit(solution)/shard_map/ppermute | solution.py:291
  60.5 1.9 %add_tiles.5 = bf16[1,512,512]{2,1,0:T(8,128)(2,1)} custom-call(s32[1,16]{1,0:T(1,128)S(1)} %copy-done.4, bf16[1,16,256,512]{3,2,1,0:T(8,128)(2,1)S(1)} %copy-done.1, bf16[512,128]{1,0:T(8,128)(2,1)S(1)} %collective-permute-done.refs_2_, bf16[512,128]{1,0:T(8,128)(2,1)S(1)} %collective-permute-done.1.refs_3_, f32[512,512]{1,0:T(8,128)S(1)} %add_tiles.4.refs_4_), custom_call_target="tpu_custom_call" | custom-call | flops 268435456 | bytes 262144 | tf_op jit(solution)/shard_map/add_tiles/pallas_call | solution.py:262
  62.4 4.5 %all-to-all-start = ((bf16[1,16,32,512]{3,2,0,1:T(8,128)(2,1)}), bf16[1,16,32,512]{3,2,0,1:T(8,128)(2,1)S(1)}, u32[]{:S(2)}, u32[]{:S(2)}) async-start(bf16[1,16,32,512]{3,2,0,1:T(8,128)(2,1)} %bitcast.1), calls=%async_computation | async-start | bytes 1048576 | tf_op jit(solution)/shard_map/all_to_all | solution.py:426
  67.7 13.5 %all-to-all-done = bf16[1,16,32,512]{3,2,0,1:T(8,128)(2,1)S(1)} async-done(((bf16[1,16,32,512]{3,2,0,1:T(8,128)(2,1)}), bf16[1,16,32,512]{3,2,0,1:T(8,128)(2,1)S(1)}, u32[]{:S(2)}, u32[]{:S(2)}) %all-to-all-start) | async-done | bytes 524320 | tf_op jit(solution)/shard_map/all_to_all | solution.py:426
  81.2 6.9 %gate.1 = bf16[16,32,64,256]{3,2,1,0:T(8,128)(2,1)} custom-call(bf16[1,16,1,32,512]{4,3,2,1,0:T(8,128)(2,1)S(1)} %bitcast.8, f32[1,16,32,1]{3,2,1,0:T(8,128)S(1)} %copy.12.cos_g_ref, f32[1,16,32,1]{3,2,1,0:T(8,128)S(1)} %copy.13.sin_g_ref, bf16[512,256]{1,0:T(8,128)(2,1)S(1)} %pad_maximum_fusion.smooth_ref, bf16[1,2,64,256]{3,2,1,0:T(8,128)(2,1)S(1)} %broadcast_in_dim.32.wave_ref), custom_call_target="tpu_custom_call" | custom-call | tf_op jit(solution)/shard_map/gate/pallas_call | solution.py:384
  (36 shorter events, 2.8 us)
Async XLA Ops:
  0.0 7.7 %copy-start.4 = (s32[1,16]{1,0:T(1,128)S(1)}, s32[1,16]{1,0:T(1,128)}, u32[]{:S(2)}) copy-start(s32[1,16]{1,0:T(1,128)} %refs_0_.5) | copy-start | bytes 196
  0.0 7.7 %copy-start.3 = (s32[1,16,16]{2,1,0:T(8,128)S(1)}, s32[1,16,16]{2,1,0:T(8,128)}, u32[]{:S(2)}) copy-start(s32[1,16,16]{2,1,0:T(8,128)} %rank_ref.3) | copy-start | bytes 3076
  0.0 7.7 %copy-start.2 = (bf16[1,512,512]{2,1,0:T(8,128)(2,1)S(1)}, bf16[1,512,512]{2,1,0:T(8,128)(2,1)}, u32[]{:S(2)}) copy-start(bf16[1,512,512]{2,1,0:T(8,128)(2,1)} %x_ref.3) | copy-start | bytes 1572868
  2.5 16.2 %collective-permute-start.2 = (bf16[512,128]{1,0:T(8,128)(2,1)}, bf16[512,128]{1,0:T(8,128)(2,1)S(1)}, u32[]{:S(2)}, u32[]{:S(2)}) collective-permute-start(bf16[512,128]{1,0:T(8,128)(2,1)} %get-tuple-element.23), channel_id=1, source_target_pairs={{0,12},{1,13},{2,14},{3,15},{4,8},{5,9},{6,10},{7,11},{8,4},{9,5},... | collective-permute-start | bytes 393224 | tf_op jit(solution)/shard_map/ppermute | solution.py:291
  7.7 12.0 %collective-permute-start.3 = (bf16[512,128]{1,0:T(8,128)(2,1)}, bf16[512,128]{1,0:T(8,128)(2,1)S(1)}, u32[]{:S(2)}, u32[]{:S(2)}) collective-permute-start(bf16[512,128]{1,0:T(8,128)(2,1)} %get-tuple-element.24), channel_id=1, source_target_pairs={{0,13},{1,12},{2,15},{3,14},{4,9},{5,8},{6,11},{7,10},{8,5},{9,4},... | collective-permute-start | bytes 393224 | tf_op jit(solution)/shard_map/ppermute | solution.py:291
  7.7 2.2 %copy-start = (bf16[1,16,512,256]{3,2,1,0:T(8,128)(2,1)S(1)}, bf16[1,16,512,256]{3,2,1,0:T(8,128)(2,1)}, u32[]{:S(2)}) copy-start(bf16[1,16,512,256]{3,2,1,0:T(8,128)(2,1)} %v_ref.3) | copy-start | bytes 12582916
  9.9 34.4 %copy-start.1 = (bf16[1,16,256,512]{3,2,1,0:T(8,128)(2,1)S(1)}, bf16[1,16,256,512]{3,2,1,0:T(8,128)(2,1)}, u32[]{:S(2)}) copy-start(bf16[1,16,256,512]{3,2,1,0:T(8,128)(2,1)} %refs_1_.5) | copy-start | bytes 12582916
  11.6 11.1 %collective-permute-start.4 = (bf16[512,128]{1,0:T(8,128)(2,1)S(1)}, bf16[512,128]{1,0:T(8,128)(2,1)S(1)}, u32[]{:S(2)}, u32[]{:S(2)}) collective-permute-start(bf16[512,128]{1,0:T(8,128)(2,1)S(1)} %get-tuple-element.25), channel_id=1, source_target_pairs={{0,14},{1,15},{2,12},{3,13},{4,10},{5,11},{6,8},{7,9},{8,6},{9,7},... | collective-permute-start | bytes 393224 | tf_op jit(solution)/shard_map/ppermute | solution.py:291
  17.5 7.3 %collective-permute-start.8 = (bf16[512,128]{1,0:T(8,128)(2,1)S(1)}, bf16[512,128]{1,0:T(8,128)(2,1)S(1)}, u32[]{:S(2)}, u32[]{:S(2)}) collective-permute-start(bf16[512,128]{1,0:T(8,128)(2,1)S(1)} %get-tuple-element.30), channel_id=1, source_target_pairs={{0,1},{1,0},{2,3},{3,2},{4,5},{5,4},{6,7},{7,6},{8,9},{9,8},{10,11... | collective-permute-start | bytes 393224 | tf_op jit(solution)/shard_map/ppermute | solution.py:291
  18.2 7.9 %collective-permute-start.9 = (bf16[512,128]{1,0:T(8,128)(2,1)S(1)}, bf16[512,128]{1,0:T(8,128)(2,1)S(1)}, u32[]{:S(2)}, u32[]{:S(2)}) collective-permute-start(bf16[512,128]{1,0:T(8,128)(2,1)S(1)} %get-tuple-element.31), channel_id=1, source_target_pairs={{0,2},{1,3},{2,0},{3,1},{4,6},{5,7},{6,4},{7,5},{8,10},{9,11},{10,... | collective-permute-start | bytes 393224 | tf_op jit(solution)/shard_map/ppermute | solution.py:291
  18.8 9.8 %collective-permute-start.10 = (bf16[512,128]{1,0:T(8,128)(2,1)S(1)}, bf16[512,128]{1,0:T(8,128)(2,1)S(1)}, u32[]{:S(2)}, u32[]{:S(2)}) collective-permute-start(bf16[512,128]{1,0:T(8,128)(2,1)S(1)} %get-tuple-element.32), channel_id=1, source_target_pairs={{0,3},{1,2},{2,1},{3,0},{4,7},{5,6},{6,5},{7,4},{8,11},{9,10},{10,... | collective-permute-start | bytes 393224 | tf_op jit(solution)/shard_map/ppermute | solution.py:291
  19.7 10.1 %collective-permute-start.11 = (bf16[512,128]{1,0:T(8,128)(2,1)S(1)}, bf16[512,128]{1,0:T(8,128)(2,1)S(1)}, u32[]{:S(2)}, u32[]{:S(2)}) collective-permute-start(bf16[512,128]{1,0:T(8,128)(2,1)S(1)} %get-tuple-element.33), channel_id=1, source_target_pairs={{0,4},{1,5},{2,6},{3,7},{4,0},{5,1},{6,2},{7,3},{8,12},{9,13},{10,... | collective-permute-start | bytes 393224 | tf_op jit(solution)/shard_map/ppermute | solution.py:291
  22.6 7.6 %collective-permute-start.12 = (bf16[512,128]{1,0:T(8,128)(2,1)S(1)}, bf16[512,128]{1,0:T(8,128)(2,1)S(1)}, u32[]{:S(2)}, u32[]{:S(2)}) collective-permute-start(bf16[512,128]{1,0:T(8,128)(2,1)S(1)} %get-tuple-element.34), channel_id=1, source_target_pairs={{0,5},{1,4},{2,7},{3,6},{4,1},{5,0},{6,3},{7,2},{8,13},{9,12},{10,... | collective-permute-start | bytes 393224 | tf_op jit(solution)/shard_map/ppermute | solution.py:291
  24.9 8.7 %collective-permute-start.13 = (bf16[512,128]{1,0:T(8,128)(2,1)S(1)}, bf16[512,128]{1,0:T(8,128)(2,1)S(1)}, u32[]{:S(2)}, u32[]{:S(2)}) collective-permute-start(bf16[512,128]{1,0:T(8,128)(2,1)S(1)} %get-tuple-element.35), channel_id=1, source_target_pairs={{0,6},{1,7},{2,4},{3,5},{4,2},{5,3},{6,0},{7,1},{8,14},{9,15},{10,... | collective-permute-start | bytes 393224 | tf_op jit(solution)/shard_map/ppermute | solution.py:291
  26.1 18.1 %collective-permute-start.14 = (bf16[512,128]{1,0:T(8,128)(2,1)S(1)}, bf16[512,128]{1,0:T(8,128)(2,1)S(1)}, u32[]{:S(2)}, u32[]{:S(2)}) collective-permute-start(bf16[512,128]{1,0:T(8,128)(2,1)S(1)} %get-tuple-element.36), channel_id=1, source_target_pairs={{0,7},{1,6},{2,5},{3,4},{4,3},{5,2},{6,1},{7,0},{8,15},{9,14},{10,... | collective-permute-start | bytes 393224 | tf_op jit(solution)/shard_map/ppermute | solution.py:291
  28.6 17.5 %collective-permute-start.5 = (bf16[512,128]{1,0:T(8,128)(2,1)S(1)}, bf16[512,128]{1,0:T(8,128)(2,1)S(1)}, u32[]{:S(2)}, u32[]{:S(2)}) collective-permute-start(bf16[512,128]{1,0:T(8,128)(2,1)S(1)} %get-tuple-element.26), channel_id=1, source_target_pairs={{0,15},{1,14},{2,13},{3,12},{4,11},{5,10},{6,9},{7,8},{8,7},{9,6},... | collective-permute-start | bytes 393224 | tf_op jit(solution)/shard_map/ppermute | solution.py:291
  29.7 16.3 %collective-permute-start.6 = (bf16[512,128]{1,0:T(8,128)(2,1)S(1)}, bf16[512,128]{1,0:T(8,128)(2,1)S(1)}, u32[]{:S(2)}, u32[]{:S(2)}) collective-permute-start(bf16[512,128]{1,0:T(8,128)(2,1)S(1)} %get-tuple-element.27), channel_id=1, source_target_pairs={{0,8},{1,9},{2,10},{3,11},{4,12},{5,13},{6,14},{7,15},{8,0},{9,1},... | collective-permute-start | bytes 393224 | tf_op jit(solution)/shard_map/ppermute | solution.py:291
  30.2 24.4 %collective-permute-start.7 = (bf16[512,128]{1,0:T(8,128)(2,1)S(1)}, bf16[512,128]{1,0:T(8,128)(2,1)S(1)}, u32[]{:S(2)}, u32[]{:S(2)}) collective-permute-start(bf16[512,128]{1,0:T(8,128)(2,1)S(1)} %get-tuple-element.28), channel_id=1, source_target_pairs={{0,9},{1,8},{2,11},{3,10},{4,13},{5,12},{6,15},{7,14},{8,1},{9,0},... | collective-permute-start | bytes 393224 | tf_op jit(solution)/shard_map/ppermute | solution.py:291
  33.5 23.8 %collective-permute-start = (bf16[512,128]{1,0:T(8,128)(2,1)S(1)}, bf16[512,128]{1,0:T(8,128)(2,1)S(1)}, u32[]{:S(2)}, u32[]{:S(2)}) collective-permute-start(bf16[512,128]{1,0:T(8,128)(2,1)S(1)} %get-tuple-element.21), channel_id=1, source_target_pairs={{0,10},{1,11},{2,8},{3,9},{4,14},{5,15},{6,12},{7,13},{8,2},{9,3},... | collective-permute-start | bytes 393224 | tf_op jit(solution)/shard_map/ppermute | solution.py:291
  44.3 16.3 %collective-permute-start.1 = (bf16[512,128]{1,0:T(8,128)(2,1)S(1)}, bf16[512,128]{1,0:T(8,128)(2,1)S(1)}, u32[]{:S(2)}, u32[]{:S(2)}) collective-permute-start(bf16[512,128]{1,0:T(8,128)(2,1)S(1)} %get-tuple-element.22), channel_id=1, source_target_pairs={{0,11},{1,10},{2,9},{3,8},{4,15},{5,14},{6,13},{7,12},{8,3},{9,2},... | collective-permute-start | bytes 393224 | tf_op jit(solution)/shard_map/ppermute | solution.py:291
  56.2 10.7 %copy-start.5 = (s32[16,32]{1,0:T(8,128)S(1)}, s32[16,32]{1,0:T(8,128)}, u32[]{:S(2)}) copy-start(s32[16,32]{1,0:T(8,128)} %param.11) | copy-start | bytes 6148
  62.4 18.8 %all-to-all-start = ((bf16[1,16,32,512]{3,2,0,1:T(8,128)(2,1)}), bf16[1,16,32,512]{3,2,0,1:T(8,128)(2,1)S(1)}, u32[]{:S(2)}, u32[]{:S(2)}) async-start(bf16[1,16,32,512]{3,2,0,1:T(8,128)(2,1)} %bitcast.1), calls=%async_computation | async-start | bytes 1048576 | tf_op jit(solution)/shard_map/all_to_all | solution.py:426

commit v4 on v2

--- a/solution.py
+++ b/solution.py
@@ -1,3 +1,4 @@
+import functools
 import math
 
 import jax
@@ -7,12 +8,15 @@
 from jax.experimental.pallas import tpu as pltpu
 from jax.sharding import PartitionSpec as P
 
+
 TC = 16
 TR = 16
 RMAX = 128
 SIDE = 16
 NT = 1024
 GT = 64
+slots = 4
+
 
 edge_weight = 0.15
 centre_weight = 0.7
@@ -119,6 +123,407 @@
         compiler_params=pltpu.CompilerParams(vmem_limit_bytes=24 * 2**20),
         name="expand",
     )(col_map, incoming, weights)
+
+
+def far_first(devices):
+    return sorted(range(1, devices), key=lambda k: (-(k >> 2), k)) + [0]
+
+
+def build_left(x, left_ref):
+    tile_len, cols = x.shape
+    sources = cols // 2
+    real_x = x[:, :sources].T
+    imag_x = x[:, sources:].T
+    left_ref[:sources, :tile_len] = real_x
+    left_ref[:sources, tile_len:] = -imag_x
+    left_ref[sources:, :tile_len] = imag_x
+    left_ref[sources:, tile_len:] = real_x
+
+
+def project_two(left_ref, tiles, ranks):
+    lane = lax.broadcasted_iota(jnp.int32, (1, 2 * RMAX), 1)
+    one, two = tiles
+    real_v = jnp.concatenate([one[:, :RMAX], two[:, :RMAX]], axis=1)
+    imag_v = jnp.concatenate([one[:, RMAX:], two[:, RMAX:]], axis=1)
+    both = matmul(left_ref[...], jnp.concatenate([real_v, imag_v], axis=0))
+    live = (lane < ranks[0]) | ((lane >= RMAX) & (lane < ranks[1] + RMAX))
+    both = jnp.where(live, both, 0.0)
+    sources = both.shape[0] // 2
+    half = RMAX // 2
+    low_lane = lax.broadcasted_iota(jnp.int32, (1, RMAX), 1) < half
+    out = []
+    for side in range(2):
+        real_z = both[:sources, side * RMAX:(side + 1) * RMAX]
+        imag_z = both[sources:, side * RMAX:(side + 1) * RMAX]
+        lower = jnp.where(low_lane, real_z, pltpu.roll(imag_z, half, axis=1))
+        upper = jnp.where(low_lane, pltpu.roll(real_z, half, axis=1), imag_z)
+        out.append((lower.astype(jnp.bfloat16), upper.astype(jnp.bfloat16)))
+    return out
+
+
+def fetch_tiles(v_hbm, tile_ref, sems, rows):
+    copies = [
+        pltpu.make_async_copy(v_hbm.at[0, row], tile_ref.at[n], sems.at[n])
+        for n, row in enumerate(rows)
+    ]
+    for copy in copies:
+        copy.start()
+    return copies
+
+
+def project_all(copies, left_ref, tile_ref, ranks):
+    out = []
+    for n in range(0, len(copies), 2):
+        copies[n].wait()
+        copies[n + 1].wait()
+        out += project_two(left_ref, [tile_ref[n], tile_ref[n + 1]], ranks[n:n + 2])
+    return out
+
+
+def project_rows(left_ref, v_ref, rows, ranks):
+    out = []
+    for n in range(0, len(rows), 2):
+        tiles = [v_ref[0, rows[n]], v_ref[0, rows[n + 1]]]
+        out += project_two(left_ref, tiles, ranks[n:n + 2])
+    return out
+
+
+def send_first_kernel(ids, rank_hbm, col_hbm, v_hbm, x_hbm, *refs):
+    count = len(ids)
+    low_refs = refs[:count]
+    left_ref, tile_ref, sems, x_ref, rank_ref, col_ref, more_sems = refs[count:]
+    device = lax.axis_index("tile")
+    rows = [jnp.bitwise_xor(device, k) for k in ids]
+    more = [
+        pltpu.make_async_copy(x_hbm.at[0], x_ref, more_sems.at[0]),
+        pltpu.make_async_copy(rank_hbm.at[0], rank_ref, more_sems.at[1]),
+        pltpu.make_async_copy(col_hbm, col_ref, more_sems.at[2]),
+    ]
+    for copy in more:
+        copy.start()
+    copies = fetch_tiles(v_hbm, tile_ref, sems, rows)
+    more[0].wait()
+    build_left(x_ref[...], left_ref)
+    more[1].wait()
+    more[2].wait()
+    column = col_ref[0, device]
+    ranks = [rank_ref[row, column] for row in rows]
+    for n, (lower, _) in enumerate(project_all(copies, left_ref, tile_ref, ranks)):
+        low_refs[n][...] = lower
+
+
+def send_far_kernel(skip, ids, rank_ref, col_ref, x_ref, v_ref, *refs):
+    count = len(ids)
+    low_refs, refs = refs[:count - skip], refs[count - skip:]
+    slot_ref, left_ref, up_ref = refs
+    device = lax.axis_index("tile")
+    column = col_ref[0, device]
+    sources = x_ref.shape[-1] // 2
+    rows = [jnp.bitwise_xor(device, k) for k in ids]
+    ranks = [rank_ref[0, row, column] for row in rows]
+    build_left(x_ref[0], left_ref)
+    for n, (lower, upper) in enumerate(project_rows(left_ref, v_ref, rows, ranks)):
+        if n >= skip:
+            low_refs[n - skip][...] = lower
+        up_ref[n] = upper
+    found = [jnp.int32(0)] * slots
+    used = jnp.int32(0)
+    for n, rank in enumerate(ranks):
+        heavy = rank > RMAX // 2
+        found = [jnp.where(heavy & (used == c), n, found[c]) for c in range(slots)]
+        used = used + heavy.astype(jnp.int32)
+    for c in range(slots):
+        tile = up_ref[found[c]]
+        slot_ref[c * sources:(c + 1) * sources] = jnp.where(
+            c < used, tile, jnp.zeros_like(tile)
+        )
+
+
+def send_near_kernel(ids, rank_ref, col_ref, x_ref, v_ref, *refs):
+    z_refs, left_ref = refs[:-1], refs[-1]
+    device = lax.axis_index("tile")
+    column = col_ref[0, device]
+    rows = [jnp.bitwise_xor(device, k) for k in ids]
+    ranks = [rank_ref[0, row, column] for row in rows]
+    sources = x_ref.shape[-1] // 2
+    build_left(x_ref[0], left_ref)
+    for n, (lower, upper) in enumerate(project_rows(left_ref, v_ref, rows, ranks)):
+        z_refs[n][:sources] = lower
+        z_refs[n][sources:] = upper
+
+
+def hand_on_kernel(far, half, rank_ref, col_ref, slot_ref, *out_refs):
+    device = lax.axis_index("tile")
+    origin = jnp.bitwise_xor(device, half)
+    column = col_ref[0, origin]
+    sources = out_refs[0].shape[0]
+    used = jnp.int32(0)
+    for k in far:
+        heavy = rank_ref[0, jnp.bitwise_xor(origin, k), column] > RMAX // 2
+        held = heavy & (used < slots)
+        at = pl.multiple_of(jnp.minimum(used, slots - 1) * sources, sources)
+        tile = slot_ref[pl.ds(at, sources)]
+        out_refs[k - half][...] = jnp.where(held, tile, jnp.zeros_like(tile))
+        used = used + heavy.astype(jnp.int32)
+
+
+def specs():
+    return (
+        pl.BlockSpec(memory_space=m) for m in (pltpu.VMEM, pltpu.SMEM, pltpu.HBM)
+    )
+
+
+def send_cost(count, v_tiles, cols):
+    tile_len, wide = v_tiles.shape[2:]
+    return pl.CostEstimate(
+        flops=4 * count * cols * tile_len * RMAX,
+        bytes_accessed=count * tile_len * wide * 2,
+        transcendentals=0,
+    )
+
+
+def tile_scratch(count, v_tiles, cols):
+    tile_len, wide = v_tiles.shape[2:]
+    return [
+        pltpu.VMEM((cols, 2 * tile_len), jnp.bfloat16),
+        pltpu.VMEM((count, tile_len, wide), jnp.bfloat16),
+        pltpu.SemaphoreType.DMA((count,)),
+    ]
+
+
+def send_first(ids, ranks, col_map, v_tiles, src_slots):
+    cols = src_slots.shape[-1]
+    count = len(ids)
+    vmem, _, hbm = specs()
+    return pl.pallas_call(
+        functools.partial(send_first_kernel, ids),
+        out_shape=[jax.ShapeDtypeStruct((cols // 2, RMAX), jnp.bfloat16)] * count,
+        in_specs=[hbm] * 4,
+        out_specs=[vmem] * count,
+        scratch_shapes=tile_scratch(count, v_tiles, cols)
+        + [
+            pltpu.VMEM(src_slots.shape[1:], jnp.bfloat16),
+            pltpu.SMEM(ranks.shape[1:], jnp.int32),
+            pltpu.SMEM(col_map.shape, jnp.int32),
+            pltpu.SemaphoreType.DMA((3,)),
+        ],
+        compiler_params=pltpu.CompilerParams(vmem_limit_bytes=60 * 2**20),
+        cost_estimate=send_cost(count, v_tiles, cols),
+        name="send_first",
+    )(ranks, col_map, v_tiles, src_slots)
+
+
+def send_far(skip, ids, ranks, col_map, v_tiles, src_slots):
+    cols = src_slots.shape[-1]
+    count = len(ids)
+    vmem, smem, _ = specs()
+    shapes = [jax.ShapeDtypeStruct((cols // 2, RMAX), jnp.bfloat16)] * (count - skip)
+    shapes.append(jax.ShapeDtypeStruct((slots * cols // 2, RMAX), jnp.bfloat16))
+    out = pl.pallas_call(
+        functools.partial(send_far_kernel, skip, ids),
+        out_shape=shapes,
+        in_specs=[smem, smem, vmem, vmem],
+        out_specs=[vmem] * len(shapes),
+        scratch_shapes=tile_scratch(count, v_tiles, cols)[:1]
+        + [pltpu.VMEM((count, cols // 2, RMAX), jnp.bfloat16)],
+        compiler_params=pltpu.CompilerParams(vmem_limit_bytes=12 * 2**20),
+        cost_estimate=send_cost(count, v_tiles, cols),
+        name="send_far",
+    )(ranks, col_map, src_slots, v_tiles)
+    return out[:-1], out[-1]
+
+
+def send_near(ids, ranks, col_map, v_tiles, src_slots):
+    cols = src_slots.shape[-1]
+    count = len(ids)
+    vmem, smem, _ = specs()
+    return pl.pallas_call(
+        functools.partial(send_near_kernel, ids),
+        out_shape=[jax.ShapeDtypeStruct((cols, RMAX), jnp.bfloat16)] * count,
+        in_specs=[smem, smem, vmem, vmem],
+        out_specs=[vmem] * count,
+        scratch_shapes=tile_scratch(count, v_tiles, cols)[:1],
+        compiler_params=pltpu.CompilerParams(vmem_limit_bytes=12 * 2**20),
+        cost_estimate=send_cost(count, v_tiles, cols),
+        name="send_near",
+    )(ranks, col_map, src_slots, v_tiles)
+
+
+def hand_on(far, half, ranks, col_map, held):
+    vmem, smem, _ = specs()
+    shape = (held.shape[0] // slots, RMAX)
+    return pl.pallas_call(
+        functools.partial(hand_on_kernel, far, half),
+        out_shape=[jax.ShapeDtypeStruct(shape, jnp.bfloat16)] * half,
+        in_specs=[smem, smem, vmem],
+        out_specs=[vmem] * half,
+        compiler_params=pltpu.CompilerParams(vmem_limit_bytes=4 * 2**20),
+        cost_estimate=pl.CostEstimate(
+            flops=0, bytes_accessed=2 * half * shape[0] * RMAX * 2, transcendentals=0
+        ),
+        name="hand_on",
+    )(ranks, col_map, held)
+
+
+def add_kernel(lows, ups, first, last, rank_ref, col_ref, u_hbm, *refs):
+    count = len(lows) + len(ups)
+    z_refs, out_ref = refs[:count], refs[count if first else count + 1]
+    total_ref, low_ref, up_ref, sems = refs[-4:]
+    sources = total_ref.shape[0]
+    tile_len = u_hbm.shape[-1]
+    device = lax.axis_index("tile")
+    half = RMAX // 2
+
+    def fetches(n, where, held_ref):
+        k, side, _ = where
+        column = col_ref[0, jnp.bitwise_xor(device, k)]
+        at = n if held_ref is low_ref else n + len(lows)
+        return [
+            pltpu.make_async_copy(
+                u_hbm.at[0, column, pl.ds(part * RMAX + side * half, half)],
+                held_ref.at[n, pl.ds(part * half, half)],
+                sems.at[at, part],
+            )
+            for part in range(2)
+        ]
+
+    def add(items, start):
+        left, real_w, imag_w = [], [], []
+        for z_ref, held_ref, n, (_, _, offset) in items:
+            real_u, imag_u = held_ref[n, :half], held_ref[n, half:]
+            left.append(z_ref[offset * sources:(offset + 1) * sources])
+            real_w += [real_u, -imag_u]
+            imag_w += [imag_u, real_u]
+        left = jnp.concatenate(left, axis=1)
+        for part, weights in enumerate((real_w, imag_w)):
+            at = slice(part * tile_len, (part + 1) * tile_len)
+            term = matmul(left, jnp.concatenate(weights, axis=0))
+            if start is None:
+                total_ref[:, at] = term
+            else:
+                total_ref[:, at] = start[:, at] + term
+
+    low_copies = [fetches(n, where, low_ref) for n, where in enumerate(lows)]
+    up_copies = [fetches(n, where, up_ref) for n, where in enumerate(ups)]
+    alive = [
+        rank_ref[0, device, col_ref[0, jnp.bitwise_xor(device, where[0])]] > half
+        for where in ups
+    ]
+    for copies in low_copies:
+        for copy in copies:
+            copy.start()
+    for copies, live in zip(up_copies, alive):
+
+        @pl.when(live)
+        def _():
+            for copy in copies:
+                copy.start()
+
+    items = [(z, low_ref, n, at) for n, (z, at) in enumerate(zip(z_refs, lows))]
+    for n in range(0, len(lows), 2):
+        for copy in low_copies[n] + low_copies[n + 1]:
+            copy.wait()
+        begin = (None if first else refs[count]) if n == 0 else total_ref
+        add(items[n:n + 2], begin)
+    for n, (z_ref, where) in enumerate(zip(z_refs[len(lows):], ups)):
+
+        @pl.when(alive[n])
+        def _():
+            for copy in up_copies[n]:
+                copy.wait()
+            add([(z_ref, up_ref, n, where)], total_ref)
+
+    if last:
+        total = total_ref[...].astype(jnp.bfloat16)
+        out_ref[0, :, :sources] = total[:, :tile_len].T
+        out_ref[0, :, sources:] = total[:, tile_len:].T
+    else:
+        out_ref[...] = total_ref[...]
+
+
+def add_tiles(lows, ups, ranks, col_map, u_tiles, sources, total=None, last=False):
+    first = total is None
+    tile_len = u_tiles.shape[-1]
+    vmem, smem, hbm = specs()
+    tiles = [tile for tile, _ in lows + ups]
+    operands = [ranks, col_map, u_tiles, *tiles] + ([] if first else [total])
+    shape = (
+        jax.ShapeDtypeStruct((1, tile_len, 2 * sources), jnp.bfloat16)
+        if last
+        else jax.ShapeDtypeStruct((sources, 2 * tile_len), jnp.float32)
+    )
+    kernel = functools.partial(
+        add_kernel, [at for _, at in lows], [at for _, at in ups], first, last
+    )
+    return pl.pallas_call(
+        kernel,
+        out_shape=shape,
+        in_specs=[smem, smem, hbm] + [vmem] * (len(operands) - 3),
+        out_specs=vmem,
+        scratch_shapes=[
+            pltpu.VMEM((sources, 2 * tile_len), jnp.float32),
+            pltpu.VMEM((len(lows), RMAX, tile_len), jnp.bfloat16),
+            pltpu.VMEM((len(ups), RMAX, tile_len), jnp.bfloat16),
+            pltpu.SemaphoreType.DMA((len(tiles), 2)),
+        ],
+        compiler_params=pltpu.CompilerParams(vmem_limit_bytes=12 * 2**20),
+        cost_estimate=pl.CostEstimate(
+            flops=4 * len(tiles) * sources * RMAX * tile_len,
+            bytes_accessed=len(tiles) * sources * RMAX * 2,
+            transcendentals=0,
+        ),
+        name="add_tiles",
+    )(*operands)
+
+
+def exchange(ranks, col_map, v_tiles, src_slots, u_tiles):
+    devices = lax.axis_size("tile")
+    half = devices // 2
+    sources = src_slots.shape[-1] // 2
+    order = far_first(devices)
+    far, near = order[:half], order[half:]
+    begin, rest = far[:2], far[2:]
+
+    def swap(value, k):
+        return lax.ppermute(value, "tile", [(d, d ^ k) for d in range(devices)])
+
+    lower = send_first(begin, ranks, col_map, v_tiles, src_slots)
+    arrived = {k: swap(tile, k) for k, tile in zip(begin, lower)}
+    lower, held = send_far(len(begin), far, ranks, col_map, v_tiles, src_slots)
+    held = swap(held, half)
+    whole = send_near(near, ranks, col_map, v_tiles, src_slots)
+    arrived.update((k, swap(tile, k) if k else tile) for k, tile in zip(near, whole))
+    arrived.update((k, swap(tile, k)) for k, tile in zip(rest, lower))
+    handed = hand_on(far, half, ranks, col_map, held)
+    uppers = {k: swap(handed[k], k) if k else handed[k] for k in near}
+
+    own = sorted(near)
+    groups = [
+        (
+            [(arrived[k], (k, 0, 0)) for k in own],
+            [(arrived[k], (k, 1, 1)) for k in own],
+        ),
+        (
+            [(arrived[k], (k, 0, 0)) for k in far],
+            [(uppers[k], (k + half, 1, 0)) for k in own],
+        ),
+    ]
+    total = None
+    for n, (lows, ups) in enumerate(groups):
+        last = n == len(groups) - 1
+        total = add_tiles(lows, ups, ranks, col_map, u_tiles, sources, total, last)
+        if n == 0:
+            late = total
+    return total, late
+
+
+def too_many(ranks, col_map, devices):
+    ids = jnp.arange(devices, dtype=jnp.int32)
+    mine = (col_map[0][:, None] == ids[None, :]).astype(jnp.int32)
+    heavy = (ranks[0] > RMAX // 2).astype(jnp.int32)
+    far = ((ids[:, None] ^ ids[None, :]) >= devices // 2).astype(jnp.int32)
+    by_slot = jnp.sum(mine[:, None, :] * heavy[None, :, :], axis=-1)
+    return jnp.any(jnp.sum(by_slot * far, axis=1) > slots)
 
 
 def split(value):
@@ -168,9 +573,10 @@
     freq_count, all_rows = y_ref.shape[:2]
     high = 16
 
-    @pl.when(pl.program_id(0) == 0)
-    def _():
-        for first in range(0, all_rows, 4):
+    for first in range(0, all_rows, 4):
+
+        @pl.when(pl.program_id(0) * rows == first)
+        def _():
             mix_rows(y_ref, cos_g_ref, sin_g_ref, smooth_ref, mix_ref, first, 4)
 
     for i in range(rows):
@@ -235,11 +641,24 @@
     receivers = tile_len // devices
     freq_ids = jnp.arange(freq_count, dtype=jnp.int32)
 
-    outgoing = project(ranks, col_map, v_tiles, src_slots, 4, turned)
-    if not turned:
-        outgoing = outgoing.reshape(devices, rank_block, cols)
-    incoming = lax.all_to_all(outgoing, "tile", split_axis=0, concat_axis=0, tiled=True)
-    partial_value = expand(col_map, incoming, u_tiles, cols, turned)
+    def all_at_once():
+        outgoing = project(ranks, col_map, v_tiles, src_slots, 4, turned)
+        if not turned:
+            outgoing = outgoing.reshape(devices, rank_block, cols)
+        incoming = lax.all_to_all(outgoing, "tile", split_axis=0, concat_axis=0, tiled=True)
+        return expand(col_map, incoming, u_tiles, cols, turned)
+
+    if turned:
+        partial_value, late = exchange(ranks, col_map, v_tiles, src_slots, u_tiles)
+        late_ranks, _ = lax.optimization_barrier((ranks, late[:8, :128]))
+        partial_value = lax.cond(
+            too_many(late_ranks, col_map, devices),
+            lambda _: all_at_once(),
+            lambda kept: kept,
+            partial_value,
+        )
+    else:
+        partial_value = all_at_once()
     spread = partial_value.reshape(freq_count, devices, receivers, cols)
     arrived = lax.all_to_all(spread, "tile", split_axis=1, concat_axis=1, tiled=True)
     arrived = arrived.reshape(freq_count, TR, blocks_per, receivers, cols)
@@ -249,7 +668,7 @@
     cos_g, sin_g = waves(gate_start, bins)
     cos_g, sin_g = scale * cos_g[..., None], scale * sin_g[..., None]
     wave = gate_waves(bins, cols // 2)
-    return gate(arrived, cos_g, sin_g, smoother(cols // 2), wave, 2)
+    return gate(arrived, cos_g, sin_g, smoother(cols // 2), wave, 4)
 
 
 def solution(mesh):

time: 91.9 us -> 92.3 us (level)
  blocking collectives: 54.8 us -> 0 us
  starting transfers between devices: 5.14 us -> 29.8 us
  waiting for transfers between devices: 13.5 us -> 36.6 us
  Pallas kernels: 17.3 us -> 22.6 us
  other arithmetic: 0.38 us -> 1.54 us
    all_to_all x1 -> x0, blocking collectives: 54.8 us -> none  [on_device(): lax.all_to_all(outgoing, 'tile', split_axis=0, concat_axis=0, tiled=True)]
    ppermute x0 -> x23, starting transfers between devices: none -> 25.9 us  [swap(): return lax.ppermute(value, 'tile', [(d, d ^ k) for d in range(devices)])]
    ppermute x0 -> x23, waiting for transfers between devices: none -> 23.1 us  [swap(): return lax.ppermute(value, 'tile', [(d, d ^ k) for d in range(devices)])]
    pallas_call x2 -> x6, Pallas kernels: 9.83 us -> 15.7 us  [the longest x2 6.72 us: add_tiles(): pl.pallas_call(kernel, out_shape=shape, in_specs=[smem, smem, hbm] + [vme...]
    all_to_all x1, starting transfers between devices: 5.14 us -> 3.91 us  [on_device(): lax.all_to_all(spread, 'tile', split_axis=1, concat_axis=1, tiled=True)]
  transfers between devices with their start and end apart: 1 -> 24, of which waited for: 1 -> 11; matrix products, arithmetic and copies ran while one was open for 1% -> 2% of each run, Pallas kernels for 0% -> 10%
where the time goes in v4:
time: 92.3 us; the launch traced here: 91.8 us
  waiting for transfers between devices  36.6 us (40%)
  starting transfers between devices  29.8 us (32%)
  Pallas kernels  22.6 us (24%)
  other arithmetic  1.54 us (2%)
    ppermute x23, starting transfers between devices, swap(): return lax.ppermute(value, 'tile', [(d, d ^ k) for d in range(devices)])  25.9 us
    ppermute x23, waiting for transfers between devices, swap(): return lax.ppermute(value, 'tile', [(d, d ^ k) for d in range(devices)])  23.1 us
    all_to_all x1, waiting for transfers between devices, on_device(): lax.all_to_all(spread, 'tile', split_axis=1, concat_axis=1, tiled=True)  13.5 us
    pallas_call x1, Pallas kernels, gate(): pl.pallas_call(gate_kernel, out_shape=jax.ShapeDtypeStruct((rows, receive...  6.87 us
    pallas_call x2, Pallas kernels, add_tiles(): pl.pallas_call(kernel, out_shape=shape, in_specs=[smem, smem, hbm] + [vme...  6.72 us
    all_to_all x1, starting transfers between devices, on_device(): lax.all_to_all(spread, 'tile', split_axis=1, concat_axis=1, tiled=True)  3.91 us
    pallas_call x1, Pallas kernels, send_far(): pl.pallas_call(functools.partial(send_far_kernel, skip, ids), out_shape=s...  3.62 us
    pallas_call x1, Pallas kernels, send_first(): pl.pallas_call(functools.partial(send_first_kernel, ids), out_shape=[jax....  2.52 us
  transfers between devices with their start and end apart: 24, of which 11 were waited for; matrix products, arithmetic and copies ran while one was open for 2% of the time, Pallas kernels for 10%

profile of v4, /device:TPU:0, one launch (start us, length us, event | category | flops | bytes accessed | tf_op | source)
XLA Modules:
  0.0 91.8 jit_solution(2205849407035271710)
XLA Ops:
  0.0 2.5 %send_first.1 = (bf16[256,128]{1,0:T(8,128)(2,1)}, bf16[256,128]{1,0:T(8,128)(2,1)}) custom-call(s32[1,16,16]{2,1,0:T(8,128)} %rank_ref.9, s32[1,16]{1,0:T(1,128)} %col_ref.9, bf16[1,16,512,256]{3,2,1,0:T(8,128)(2,1)} %v_ref.3, bf16[1,512,512]{2,1,0:T(8,128)(2,1)} %x_ref.3), custom_call_target="tpu_custom_call" | custom-call | flops 268435456 | bytes 524288 | tf_op jit(solution)/shard_map/send_first/pallas_call | solution.py:298
  2.5 5.1 %collective-permute-start = (bf16[256,128]{1,0:T(8,128)(2,1)}, bf16[256,128]{1,0:T(8,128)(2,1)S(1)}, u32[]{:S(2)}, u32[]{:S(2)}) collective-permute-start(bf16[256,128]{1,0:T(8,128)(2,1)} %get-tuple-element.49), channel_id=1, source_target_pairs={{0,12},{1,13},{2,14},{3,15},{4,8},{5,9},{6,10},{7,11},{8,4},{9,5},... | collective-permute-start | bytes 196616 | tf_op jit(solution)/shard_map/ppermute | solution.py:488
  7.7 3.6 %send_far.1 = (bf16[256,128]{1,0:T(8,128)(2,1)S(1)}, bf16[256,128]{1,0:T(8,128)(2,1)S(1)}, bf16[256,128]{1,0:T(8,128)(2,1)S(1)}, bf16[256,128]{1,0:T(8,128)(2,1)...) custom-call(s32[1,16,16]{2,1,0:T(8,128)S(1)} %copy-done.2, ...), custom_call_target="tpu_custom_call" | custom-call | flops 1073741824 | bytes 2097152 | tf_op jit(solution)/shard_map/send_far/pallas_call | solution.py:322
  11.3 4.0 %collective-permute-start.2 = (bf16[256,128]{1,0:T(8,128)(2,1)S(1)}, bf16[256,128]{1,0:T(8,128)(2,1)S(1)}, u32[]{:S(2)}, u32[]{:S(2)}) collective-permute-start(bf16[256,128]{1,0:T(8,128)(2,1)S(1)} %get-tuple-element.51), channel_id=1, source_target_pairs={{0,14},{1,15},{2,12},{3,13},{4,10},{5,11},{6,8},{7,9},{8,6},{9,7},... | collective-permute-start | bytes 196616 | tf_op jit(solution)/shard_map/ppermute | solution.py:488
  16.0 2.5 %collective-permute-start.5 = (bf16[256,128]{1,0:T(8,128)(2,1)S(1)}, bf16[256,128]{1,0:T(8,128)(2,1)S(1)}, u32[]{:S(2)}, u32[]{:S(2)}) collective-permute-start(bf16[256,128]{1,0:T(8,128)(2,1)S(1)} %get-tuple-element.54), channel_id=1, source_target_pairs={{0,9},{1,8},{2,11},{3,10},{4,13},{5,12},{6,15},{7,14},{8,1},{9,0},... | collective-permute-start | bytes 196616 | tf_op jit(solution)/shard_map/ppermute | solution.py:488
  18.5 2.0 %send_near.1 = (bf16[512,128]{1,0:T(8,128)(2,1)S(1)}, bf16[512,128]{1,0:T(8,128)(2,1)S(1)}, bf16[512,128]{1,0:T(8,128)(2,1)S(1)}, bf16[512,128]{1,0:T(8,128)(2,1...) custom-call(s32[1,16,16]{2,1,0:T(8,128)S(1)} %copy-done.2, ...), custom_call_target="tpu_custom_call" | custom-call | flops 1073741824 | bytes 2097152 | tf_op jit(solution)/shard_map/send_near/pallas_call | solution.py:340
  20.5 1.4 %collective-permute-start.6 = (bf16[256,128]{1,0:T(8,128)(2,1)S(1)}, bf16[256,128]{1,0:T(8,128)(2,1)S(1)}, u32[]{:S(2)}, u32[]{:S(2)}) collective-permute-start(bf16[256,128]{1,0:T(8,128)(2,1)S(1)} %get-tuple-element.55), channel_id=1, source_target_pairs={{0,10},{1,11},{2,8},{3,9},{4,14},{5,15},{6,12},{7,13},{8,2},{9,3},... | collective-permute-start | bytes 196616 | tf_op jit(solution)/shard_map/ppermute | solution.py:488
  21.9 2.4 %collective-permute-start.7 = (bf16[256,128]{1,0:T(8,128)(2,1)S(1)}, bf16[256,128]{1,0:T(8,128)(2,1)S(1)}, u32[]{:S(2)}, u32[]{:S(2)}) collective-permute-start(bf16[256,128]{1,0:T(8,128)(2,1)S(1)} %get-tuple-element.56), channel_id=1, source_target_pairs={{0,11},{1,10},{2,9},{3,8},{4,15},{5,14},{6,13},{7,12},{8,3},{9,2},... | collective-permute-start | bytes 196616 | tf_op jit(solution)/shard_map/ppermute | solution.py:488
  25.8 2.0 %collective-permute-done.5.refs_5_ = bf16[256,128]{1,0:T(8,128)(2,1)S(1)} collective-permute-done((bf16[256,128]{1,0:T(8,128)(2,1)S(1)}, bf16[256,128]{1,0:T(8,128)(2,1)S(1)}, u32[]{:S(2)}, u32[]{:S(2)}) %collective-permute-start.5) | collective-permute-done | bytes 65568 | tf_op jit(solution)/shard_map/ppermute | solution.py:488
  27.7 1.5 %collective-permute-start.17 = (bf16[512,128]{1,0:T(8,128)(2,1)S(1)}, bf16[512,128]{1,0:T(8,128)(2,1)S(1)}, u32[]{:S(2)}, u32[]{:S(2)}) collective-permute-start(bf16[512,128]{1,0:T(8,128)(2,1)S(1)} %get-tuple-element.68), channel_id=1, source_target_pairs={{0,2},{1,3},{2,0},{3,1},{4,6},{5,7},{6,4},{7,5},{8,10},{9,11},{10,... | collective-permute-start | bytes 393224 | tf_op jit(solution)/shard_map/ppermute | solution.py:488
  29.3 8.6 %collective-permute-done.6.refs_6_ = bf16[256,128]{1,0:T(8,128)(2,1)S(1)} collective-permute-done((bf16[256,128]{1,0:T(8,128)(2,1)S(1)}, bf16[256,128]{1,0:T(8,128)(2,1)S(1)}, u32[]{:S(2)}, u32[]{:S(2)}) %collective-permute-start.6) | collective-permute-done | bytes 65568 | tf_op jit(solution)/shard_map/ppermute | solution.py:488
  38.9 2.0 %collective-permute-start.20 = (bf16[512,128]{1,0:T(8,128)(2,1)S(1)}, bf16[512,128]{1,0:T(8,128)(2,1)S(1)}, u32[]{:S(2)}, u32[]{:S(2)}) collective-permute-start(bf16[512,128]{1,0:T(8,128)(2,1)S(1)} %get-tuple-element.71), channel_id=1, source_target_pairs={{0,5},{1,4},{2,7},{3,6},{4,1},{5,0},{6,3},{7,2},{8,13},{9,12},{10,... | collective-permute-start | bytes 393224 | tf_op jit(solution)/shard_map/ppermute | solution.py:488
  41.6 2.1 %collective-permute-done.8.slot_ref = bf16[1024,128]{1,0:T(8,128)(2,1)S(1)} collective-permute-done((bf16[1024,128]{1,0:T(8,128)(2,1)S(1)}, bf16[1024,128]{1,0:T(8,128)(2,1)S(1)}, u32[]{:S(2)}, u32[]{:S(2)}) %collective-permute-start.8) | collective-permute-done | bytes 262176 | tf_op jit(solution)/shard_map/ppermute | solution.py:488
  45.0 1.4 %collective-permute-done.19.refs_4_.refs_12_ = bf16[512,128]{1,0:T(8,128)(2,1)S(1)} collective-permute-done((bf16[512,128]{1,0:T(8,128)(2,1)S(1)}, bf16[512,128]{1,0:T(8,128)(2,1)S(1)}, u32[]{:S(2)}, u32[]{:S(2)}) %collective-permute-start.19) | collective-permute-done | bytes 131104 | tf_op jit(solution)/shard_map/ppermute | solution.py:488
  46.4 1.5 %collective-permute-start.10 = (bf16[256,128]{1,0:T(8,128)(2,1)S(1)}, bf16[256,128]{1,0:T(8,128)(2,1)S(1)}, u32[]{:S(2)}, u32[]{:S(2)}) collective-permute-start(bf16[256,128]{1,0:T(8,128)(2,1)S(1)} %get-tuple-element.60), channel_id=1, source_target_pairs={{0,2},{1,3},{2,0},{3,1},{4,6},{5,7},{6,4},{7,5},{8,10},{9,11},{10,... | collective-permute-start | bytes 196616 | tf_op jit(solution)/shard_map/ppermute | solution.py:488
  49.2 1.2 %collective-permute-start.11 = (bf16[256,128]{1,0:T(8,128)(2,1)S(1)}, bf16[256,128]{1,0:T(8,128)(2,1)S(1)}, u32[]{:S(2)}, u32[]{:S(2)}) collective-permute-start(bf16[256,128]{1,0:T(8,128)(2,1)S(1)} %get-tuple-element.61), channel_id=1, source_target_pairs={{0,3},{1,2},{2,1},{3,0},{4,7},{5,6},{6,5},{7,4},{8,11},{9,10},{10,... | collective-permute-start | bytes 196616 | tf_op jit(solution)/shard_map/ppermute | solution.py:488
  50.5 2.6 %collective-permute-done.21.refs_6_.refs_14_ = bf16[512,128]{1,0:T(8,128)(2,1)S(1)} collective-permute-done((bf16[512,128]{1,0:T(8,128)(2,1)S(1)}, bf16[512,128]{1,0:T(8,128)(2,1)S(1)}, u32[]{:S(2)}, u32[]{:S(2)}) %collective-permute-start.21) | collective-permute-done | bytes 131104 | tf_op jit(solution)/shard_map/ppermute | solution.py:488
  53.1 2.8 %collective-permute-done.22.refs_7_.refs_15_ = bf16[512,128]{1,0:T(8,128)(2,1)S(1)} collective-permute-done((bf16[512,128]{1,0:T(8,128)(2,1)S(1)}, bf16[512,128]{1,0:T(8,128)(2,1)S(1)}, u32[]{:S(2)}, u32[]{:S(2)}) %collective-permute-start.22) | collective-permute-done | bytes 131104 | tf_op jit(solution)/shard_map/ppermute | solution.py:488
  55.9 1.6 %collective-permute-start.14 = (bf16[256,128]{1,0:T(8,128)(2,1)S(1)}, bf16[256,128]{1,0:T(8,128)(2,1)S(1)}, u32[]{:S(2)}, u32[]{:S(2)}) collective-permute-start(bf16[256,128]{1,0:T(8,128)(2,1)S(1)} %get-tuple-element.64), channel_id=1, source_target_pairs={{0,6},{1,7},{2,4},{3,5},{4,2},{5,3},{6,0},{7,1},{8,14},{9,15},{10,... | collective-permute-start | bytes 196616 | tf_op jit(solution)/shard_map/ppermute | solution.py:488
  58.2 2.9 %add_tiles.2.refs_16_ = f32[256,1024]{1,0:T(8,128)S(1)} custom-call(s32[1,16,16]{2,1,0:T(8,128)S(1)} %copy-done.2, s32[1,16]{1,0:T(1,128)S(1)} %copy-done.3, bf16[1,16,256,512]{3,2,1,0:T(8,128)(2,1)} %u_hbm.3, bf16[512,128]{1,0:T(8,128)(2,1)S(1)} %get-tuple-element.66.refs_0_.refs_8_, bf16[512,128]{1,0:T(8,128)(2,1)S(1)} %collective-permute-done.16.refs_1_.refs_9_, ...), custom_call_target="tpu_custom_call" | custom-call | flops 1073741824 | bytes 1048576 | tf_op jit(solution)/shard_map/add_tiles/pallas_call | solution.py:458
  62.8 3.9 %add_tiles.3 = bf16[1,512,512]{2,1,0:T(8,128)(2,1)} custom-call(s32[1,16,16]{2,1,0:T(8,128)S(1)} %copy-done.2, s32[1,16]{1,0:T(1,128)S(1)} %copy-done.3, bf16[1,16,256,512]{3,2,1,0:T(8,128)(2,1)} %u_hbm.3, bf16[256,128]{1,0:T(8,128)(2,1)S(1)} %collective-permute-done.refs_0_, bf16[256,128]{1,0:T(8,128)(2,1)S(1)} %collective-permute-done.1.refs_1_, ...), custom_call_target="tpu_custom_call" | custom-call | flops 1073741824 | bytes 1048576 | tf_op jit(solution)/shard_map/add_tiles/pallas_call | solution.py:458
  66.7 3.9 %all-to-all-start.1 = ((bf16[1,16,32,512]{3,2,0,1:T(8,128)(2,1)}), bf16[1,16,32,512]{3,2,0,1:T(8,128)(2,1)S(1)}, u32[]{:S(2)}, u32[]{:S(2)}) async-start(bf16[1,16,32,512]{3,2,0,1:T(8,128)(2,1)} %bitcast.3), calls=%async_computation.1 | async-start | bytes 1048576 | tf_op jit(solution)/shard_map/all_to_all | solution.py:663
  71.4 13.5 %all-to-all-done.1 = bf16[1,16,32,512]{3,2,0,1:T(8,128)(2,1)S(1)} async-done(((bf16[1,16,32,512]{3,2,0,1:T(8,128)(2,1)}), bf16[1,16,32,512]{3,2,0,1:T(8,128)(2,1)S(1)}, u32[]{:S(2)}, u32[]{:S(2)}) %all-to-all-start.1) | async-done | bytes 524320 | tf_op jit(solution)/shard_map/all_to_all | solution.py:663
  85.0 6.9 %gate.1 = bf16[16,32,64,256]{3,2,1,0:T(8,128)(2,1)} custom-call(bf16[1,16,1,32,512]{4,3,2,1,0:T(8,128)(2,1)S(1)} %bitcast.11, f32[1,16,32,1]{3,2,1,0:T(8,128)S(1)} %copy.13.cos_g_ref, f32[1,16,32,1]{3,2,1,0:T(8,128)S(1)} %copy.14.sin_g_ref, bf16[512,256]{1,0:T(8,128)(2,1)S(1)} %pad_maximum_fusion.smooth_ref, ...), custom_call_target="tpu_custom_call" | custom-call | tf_op jit(solution)/shard_map/gate/pallas_call | solution.py:610
  (56 shorter events, 9.0 us)
Async XLA Ops:
  2.5 13.4 %collective-permute-start = (bf16[256,128]{1,0:T(8,128)(2,1)}, bf16[256,128]{1,0:T(8,128)(2,1)S(1)}, u32[]{:S(2)}, u32[]{:S(2)}) collective-permute-start(bf16[256,128]{1,0:T(8,128)(2,1)} %get-tuple-element.49), channel_id=1, source_target_pairs={{0,12},{1,13},{2,14},{3,15},{4,8},{5,9},{6,10},{7,11},{8,4},{9,5},... | collective-permute-start | bytes 196616 | tf_op jit(solution)/shard_map/ppermute | solution.py:488
  7.7 12.8 %collective-permute-start.1 = (bf16[256,128]{1,0:T(8,128)(2,1)}, bf16[256,128]{1,0:T(8,128)(2,1)S(1)}, u32[]{:S(2)}, u32[]{:S(2)}) collective-permute-start(bf16[256,128]{1,0:T(8,128)(2,1)} %get-tuple-element.50), channel_id=1, source_target_pairs={{0,13},{1,12},{2,15},{3,14},{4,9},{5,8},{6,11},{7,10},{8,5},{9,4},... | collective-permute-start | bytes 196616 | tf_op jit(solution)/shard_map/ppermute | solution.py:488
  11.3 10.6 %collective-permute-start.2 = (bf16[256,128]{1,0:T(8,128)(2,1)S(1)}, bf16[256,128]{1,0:T(8,128)(2,1)S(1)}, u32[]{:S(2)}, u32[]{:S(2)}) collective-permute-start(bf16[256,128]{1,0:T(8,128)(2,1)S(1)} %get-tuple-element.51), channel_id=1, source_target_pairs={{0,14},{1,15},{2,12},{3,13},{4,10},{5,11},{6,8},{7,9},{8,6},{9,7},... | collective-permute-start | bytes 196616 | tf_op jit(solution)/shard_map/ppermute | solution.py:488
  15.3 9.0 %collective-permute-start.3 = (bf16[256,128]{1,0:T(8,128)(2,1)S(1)}, bf16[256,128]{1,0:T(8,128)(2,1)S(1)}, u32[]{:S(2)}, u32[]{:S(2)}) collective-permute-start(bf16[256,128]{1,0:T(8,128)(2,1)S(1)} %get-tuple-element.52), channel_id=1, source_target_pairs={{0,15},{1,14},{2,13},{3,12},{4,11},{5,10},{6,9},{7,8},{8,7},{9,6},... | collective-permute-start | bytes 196616 | tf_op jit(solution)/shard_map/ppermute | solution.py:488
  16.0 9.8 %collective-permute-start.4 = (bf16[256,128]{1,0:T(8,128)(2,1)S(1)}, bf16[256,128]{1,0:T(8,128)(2,1)S(1)}, u32[]{:S(2)}, u32[]{:S(2)}) collective-permute-start(bf16[256,128]{1,0:T(8,128)(2,1)S(1)} %get-tuple-element.53), channel_id=1, source_target_pairs={{0,8},{1,9},{2,10},{3,11},{4,12},{5,13},{6,14},{7,15},{8,0},{9,1},... | collective-permute-start | bytes 196616 | tf_op jit(solution)/shard_map/ppermute | solution.py:488
  16.0 11.8 %collective-permute-start.5 = (bf16[256,128]{1,0:T(8,128)(2,1)S(1)}, bf16[256,128]{1,0:T(8,128)(2,1)S(1)}, u32[]{:S(2)}, u32[]{:S(2)}) collective-permute-start(bf16[256,128]{1,0:T(8,128)(2,1)S(1)} %get-tuple-element.54), channel_id=1, source_target_pairs={{0,9},{1,8},{2,11},{3,10},{4,13},{5,12},{6,15},{7,14},{8,1},{9,0},... | collective-permute-start | bytes 196616 | tf_op jit(solution)/shard_map/ppermute | solution.py:488
  20.5 17.4 %collective-permute-start.6 = (bf16[256,128]{1,0:T(8,128)(2,1)S(1)}, bf16[256,128]{1,0:T(8,128)(2,1)S(1)}, u32[]{:S(2)}, u32[]{:S(2)}) collective-permute-start(bf16[256,128]{1,0:T(8,128)(2,1)S(1)} %get-tuple-element.55), channel_id=1, source_target_pairs={{0,10},{1,11},{2,8},{3,9},{4,14},{5,15},{6,12},{7,13},{8,2},{9,3},... | collective-permute-start | bytes 196616 | tf_op jit(solution)/shard_map/ppermute | solution.py:488
  21.9 16.6 %collective-permute-start.7 = (bf16[256,128]{1,0:T(8,128)(2,1)S(1)}, bf16[256,128]{1,0:T(8,128)(2,1)S(1)}, u32[]{:S(2)}, u32[]{:S(2)}) collective-permute-start(bf16[256,128]{1,0:T(8,128)(2,1)S(1)} %get-tuple-element.56), channel_id=1, source_target_pairs={{0,11},{1,10},{2,9},{3,8},{4,15},{5,14},{6,13},{7,12},{8,3},{9,2},... | collective-permute-start | bytes 196616 | tf_op jit(solution)/shard_map/ppermute | solution.py:488
  24.3 19.4 %collective-permute-start.8 = (bf16[1024,128]{1,0:T(8,128)(2,1)S(1)}, bf16[1024,128]{1,0:T(8,128)(2,1)S(1)}, u32[]{:S(2)}, u32[]{:S(2)}) collective-permute-start(bf16[1024,128]{1,0:T(8,128)(2,1)S(1)} %get-tuple-element.57), channel_id=1, source_target_pairs={{0,8},{1,9},{2,10},{3,11},{4,12},{5,13},{6,14},{7,15},{8,0},{9,1},... | collective-permute-start | bytes 786440 | tf_op jit(solution)/shard_map/ppermute | solution.py:488
  25.8 13.2 %collective-permute-start.16 = (bf16[512,128]{1,0:T(8,128)(2,1)S(1)}, bf16[512,128]{1,0:T(8,128)(2,1)S(1)}, u32[]{:S(2)}, u32[]{:S(2)}) collective-permute-start(bf16[512,128]{1,0:T(8,128)(2,1)S(1)} %get-tuple-element.67), channel_id=1, source_target_pairs={{0,1},{1,0},{2,3},{3,2},{4,5},{5,4},{6,7},{7,6},{8,9},{9,8},{10,11... | collective-permute-start | bytes 393224 | tf_op jit(solution)/shard_map/ppermute | solution.py:488
  27.7 13.2 %collective-permute-start.17 = (bf16[512,128]{1,0:T(8,128)(2,1)S(1)}, bf16[512,128]{1,0:T(8,128)(2,1)S(1)}, u32[]{:S(2)}, u32[]{:S(2)}) collective-permute-start(bf16[512,128]{1,0:T(8,128)(2,1)S(1)} %get-tuple-element.68), channel_id=1, source_target_pairs={{0,2},{1,3},{2,0},{3,1},{4,6},{5,7},{6,4},{7,5},{8,10},{9,11},{10,... | collective-permute-start | bytes 393224 | tf_op jit(solution)/shard_map/ppermute | solution.py:488
  38.0 6.7 %collective-permute-start.18 = (bf16[512,128]{1,0:T(8,128)(2,1)S(1)}, bf16[512,128]{1,0:T(8,128)(2,1)S(1)}, u32[]{:S(2)}, u32[]{:S(2)}) collective-permute-start(bf16[512,128]{1,0:T(8,128)(2,1)S(1)} %get-tuple-element.69), channel_id=1, source_target_pairs={{0,3},{1,2},{2,1},{3,0},{4,7},{5,6},{6,5},{7,4},{8,11},{9,10},{10,... | collective-permute-start | bytes 393224 | tf_op jit(solution)/shard_map/ppermute | solution.py:488
  38.6 7.9 %collective-permute-start.19 = (bf16[512,128]{1,0:T(8,128)(2,1)S(1)}, bf16[512,128]{1,0:T(8,128)(2,1)S(1)}, u32[]{:S(2)}, u32[]{:S(2)}) collective-permute-start(bf16[512,128]{1,0:T(8,128)(2,1)S(1)} %get-tuple-element.70), channel_id=1, source_target_pairs={{0,4},{1,5},{2,6},{3,7},{4,0},{5,1},{6,2},{7,3},{8,12},{9,13},{10,... | collective-permute-start | bytes 393224 | tf_op jit(solution)/shard_map/ppermute | solution.py:488
  38.9 10.3 %collective-permute-start.20 = (bf16[512,128]{1,0:T(8,128)(2,1)S(1)}, bf16[512,128]{1,0:T(8,128)(2,1)S(1)}, u32[]{:S(2)}, u32[]{:S(2)}) collective-permute-start(bf16[512,128]{1,0:T(8,128)(2,1)S(1)} %get-tuple-element.71), channel_id=1, source_target_pairs={{0,5},{1,4},{2,7},{3,6},{4,1},{5,0},{6,3},{7,2},{8,13},{9,12},{10,... | collective-permute-start | bytes 393224 | tf_op jit(solution)/shard_map/ppermute | solution.py:488
  41.0 12.1 %collective-permute-start.21 = (bf16[512,128]{1,0:T(8,128)(2,1)S(1)}, bf16[512,128]{1,0:T(8,128)(2,1)S(1)}, u32[]{:S(2)}, u32[]{:S(2)}) collective-permute-start(bf16[512,128]{1,0:T(8,128)(2,1)S(1)} %get-tuple-element.72), channel_id=1, source_target_pairs={{0,6},{1,7},{2,4},{3,5},{4,2},{5,3},{6,0},{7,1},{8,14},{9,15},{10,... | collective-permute-start | bytes 393224 | tf_op jit(solution)/shard_map/ppermute | solution.py:488
  43.7 12.2 %collective-permute-start.22 = (bf16[512,128]{1,0:T(8,128)(2,1)S(1)}, bf16[512,128]{1,0:T(8,128)(2,1)S(1)}, u32[]{:S(2)}, u32[]{:S(2)}) collective-permute-start(bf16[512,128]{1,0:T(8,128)(2,1)S(1)} %get-tuple-element.73), channel_id=1, source_target_pairs={{0,7},{1,6},{2,5},{3,4},{4,3},{5,2},{6,1},{7,0},{8,15},{9,14},{10,... | collective-permute-start | bytes 393224 | tf_op jit(solution)/shard_map/ppermute | solution.py:488
  44.7 11.3 %collective-permute-start.9 = (bf16[256,128]{1,0:T(8,128)(2,1)S(1)}, bf16[256,128]{1,0:T(8,128)(2,1)S(1)}, u32[]{:S(2)}, u32[]{:S(2)}) collective-permute-start(bf16[256,128]{1,0:T(8,128)(2,1)S(1)} %get-tuple-element.59), channel_id=1, source_target_pairs={{0,1},{1,0},{2,3},{3,2},{4,5},{5,4},{6,7},{7,6},{8,9},{9,8},{10,11... | collective-permute-start | bytes 196616 | tf_op jit(solution)/shard_map/ppermute | solution.py:488
  46.4 11.1 %collective-permute-start.10 = (bf16[256,128]{1,0:T(8,128)(2,1)S(1)}, bf16[256,128]{1,0:T(8,128)(2,1)S(1)}, u32[]{:S(2)}, u32[]{:S(2)}) collective-permute-start(bf16[256,128]{1,0:T(8,128)(2,1)S(1)} %get-tuple-element.60), channel_id=1, source_target_pairs={{0,2},{1,3},{2,0},{3,1},{4,6},{5,7},{6,4},{7,5},{8,10},{9,11},{10,... | collective-permute-start | bytes 196616 | tf_op jit(solution)/shard_map/ppermute | solution.py:488
  49.2 11.9 %collective-permute-start.11 = (bf16[256,128]{1,0:T(8,128)(2,1)S(1)}, bf16[256,128]{1,0:T(8,128)(2,1)S(1)}, u32[]{:S(2)}, u32[]{:S(2)}) collective-permute-start(bf16[256,128]{1,0:T(8,128)(2,1)S(1)} %get-tuple-element.61), channel_id=1, source_target_pairs={{0,3},{1,2},{2,1},{3,0},{4,7},{5,6},{6,5},{7,4},{8,11},{9,10},{10,... | collective-permute-start | bytes 196616 | tf_op jit(solution)/shard_map/ppermute | solution.py:488
  53.1 8.0 %collective-permute-start.12 = (bf16[256,128]{1,0:T(8,128)(2,1)S(1)}, bf16[256,128]{1,0:T(8,128)(2,1)S(1)}, u32[]{:S(2)}, u32[]{:S(2)}) collective-permute-start(bf16[256,128]{1,0:T(8,128)(2,1)S(1)} %get-tuple-element.62), channel_id=1, source_target_pairs={{0,4},{1,5},{2,6},{3,7},{4,0},{5,1},{6,2},{7,3},{8,12},{9,13},{10,... | collective-permute-start | bytes 196616 | tf_op jit(solution)/shard_map/ppermute | solution.py:488
  55.9 5.2 %collective-permute-start.13 = (bf16[256,128]{1,0:T(8,128)(2,1)S(1)}, bf16[256,128]{1,0:T(8,128)(2,1)S(1)}, u32[]{:S(2)}, u32[]{:S(2)}) collective-permute-start(bf16[256,128]{1,0:T(8,128)(2,1)S(1)} %get-tuple-element.63), channel_id=1, source_target_pairs={{0,5},{1,4},{2,7},{3,6},{4,1},{5,0},{6,3},{7,2},{8,13},{9,12},{10,... | collective-permute-start | bytes 196616 | tf_op jit(solution)/shard_map/ppermute | solution.py:488
  55.9 5.9 %collective-permute-start.14 = (bf16[256,128]{1,0:T(8,128)(2,1)S(1)}, bf16[256,128]{1,0:T(8,128)(2,1)S(1)}, u32[]{:S(2)}, u32[]{:S(2)}) collective-permute-start(bf16[256,128]{1,0:T(8,128)(2,1)S(1)} %get-tuple-element.64), channel_id=1, source_target_pairs={{0,6},{1,7},{2,4},{3,5},{4,2},{5,3},{6,0},{7,1},{8,14},{9,15},{10,... | collective-permute-start | bytes 196616 | tf_op jit(solution)/shard_map/ppermute | solution.py:488
  57.5 5.3 %collective-permute-start.15 = (bf16[256,128]{1,0:T(8,128)(2,1)S(1)}, bf16[256,128]{1,0:T(8,128)(2,1)S(1)}, u32[]{:S(2)}, u32[]{:S(2)}) collective-permute-start(bf16[256,128]{1,0:T(8,128)(2,1)S(1)} %get-tuple-element.65), channel_id=1, source_target_pairs={{0,7},{1,6},{2,5},{3,4},{4,3},{5,2},{6,1},{7,0},{8,15},{9,14},{10,... | collective-permute-start | bytes 196616 | tf_op jit(solution)/shard_map/ppermute | solution.py:488
  66.7 18.2 %all-to-all-start.1 = ((bf16[1,16,32,512]{3,2,0,1:T(8,128)(2,1)}), bf16[1,16,32,512]{3,2,0,1:T(8,128)(2,1)S(1)}, u32[]{:S(2)}, u32[]{:S(2)}) async-start(bf16[1,16,32,512]{3,2,0,1:T(8,128)(2,1)} %bitcast.3), calls=%async_computation.1 | async-start | bytes 1048576 | tf_op jit(solution)/shard_map/all_to_all | solution.py:663
  (5 other events, 43.0 us)
